TPU v7x, 32 devices: a whole 2x2x4 slice. The times are simulated.
32 devices in a mesh: scene: 8 (over z, x), tie: 4 (over y, core).
Axes of the slice: x: 2, y: 2, z: 4, core: 2. Of those that a mesh axis runs over, the one named last changes fastest.
Arguments:
- tie_rows: bfloat16 [384, 256, 256], P('tie'), may hold values from -0.375 to 0.375
- point_counts: int32 [384], P('tie'), may hold values from 1 to 128, as said below
- pattern: int32 [128, 384], P('scene', 'tie'), may hold values 0 or 1
- sensitivity: bfloat16 [128, 192, 192], P('scene'), may hold values from -0.119628906 to 0.119628906
- damping: float32 [128], P(('scene', 'tie')), may hold values from 1 to 8
- prior: float32 [64], replicated, may hold values from 0.25 to 4
Outputs:
- scene_rows: float32 [128, 192, 256], P(('scene', 'tie'))
- global_factor: float32 [64, 64], replicated
Inputs may be any that keep to these rules, and one draw needn't show every extreme that they name: `point_counts`: points present in each block; some block is full.
All inputs are finite; a program needn't handle non-finite values. No bound on the sum of `pattern` on one device may be relied on, other than what follows from the above.
Results may differ from a plain program's by a relative error of at most 0.0003.
Values sent between devices are 32-bit elements; how exact they have to be, the bound alone decides.
A program may use at most 128 MiB of HBM per device.

v0:
```python
import functools
import math

import jax
import jax.numpy as jnp
from jax import lax
from jax.experimental import pallas as pl
from jax.experimental.pallas import tpu as pltpu
from jax.sharding import PartitionSpec as P

MESH = pl.DeviceIdType.MESH
HIGHEST = lax.Precision.HIGHEST
F32 = jnp.float32
BF16 = jnp.bfloat16
PANEL = 32
LANES = 128
VMEM = pl.BlockSpec(memory_space=pltpu.VMEM)


def over_rows(a, b, precision=None):
    return lax.dot_general(
        a, b, (((0,), (0,)), ((), ())), precision=precision, preferred_element_type=F32
    )


def gram_kernel(chunk, most, counts, order, active, rows_ref, out_ref, gram_ref):
    step = pl.program_id(0)

    @pl.when(step == 0)
    def _():
        out_ref[...] = jnp.zeros_like(out_ref)

    half = rows_ref.shape[2] // 2
    row_index = lax.broadcasted_iota(jnp.int32, rows_ref.shape[1:], 0)
    for i in range(chunk):
        rows = rows_ref[i]
        valid = jnp.where(row_index < 2 * counts[step * chunk + i], 1.0, 0.0).astype(BF16)
        kept = rows * valid
        top = over_rows(kept[:, :half], rows)
        gram_ref[i, :half] = top[:, :half]
        gram_ref[i, half : 2 * half] = top[:, half:]
        gram_ref[i, 2 * half :] = over_rows(kept[:, half:], rows[:, half:])
    for i in range(chunk):
        block = step * chunk + i

        def add(k, carry, i=i, block=block):
            scene = order[block * most + k]
            out_ref[scene] += gram_ref[i]
            return carry

        lax.fori_loop(0, active[block], add, 0)


def merged_partials(tie_rows, point_counts, pattern):
    blocks, rows, width = tie_rows.shape
    scenes = pattern.shape[0]
    half = width // 2
    chunk = math.gcd(blocks, 8)
    index = jnp.arange(scenes)
    seen = (pattern != 0).astype(jnp.int32).T
    before = jnp.sum(seen[:, None, :] * (index[None, :] < index[:, None])[None], 2)
    hits = (before[:, :, None] == index) & (seen[:, :, None] != 0)
    order = jnp.sum(jnp.where(hits, index[None, :, None], 0), 1).reshape(-1)
    return pl.pallas_call(
        functools.partial(gram_kernel, chunk, scenes),
        grid_spec=pltpu.PrefetchScalarGridSpec(
            num_scalar_prefetch=3,
            grid=(blocks // chunk,),
            in_specs=[pl.BlockSpec((chunk, rows, width), lambda i, *_: (i, 0, 0))],
            out_specs=pl.BlockSpec((scenes, 3 * half, half), lambda i, *_: (0, 0, 0)),
            scratch_shapes=[pltpu.VMEM((chunk, 3 * half, half), F32)],
        ),
        out_shape=jax.ShapeDtypeStruct((scenes, 3 * half, half), F32),
        name="grams",
    )(point_counts, order.astype(jnp.int32), jnp.sum(seen, 1), tie_rows)


def scatter_kernel(n, own, part, out, got, summed, far, s1, r1, s2, r2):
    me = lax.axis_index("tie")
    pairs = n // 2
    parity = lax.rem(me, 2)
    group = me // 2
    partner = me + 1 - 2 * parity

    def member(k, side):
        return lax.rem(group + k, pairs) * 2 + side

    barrier = pltpu.get_barrier_semaphore()
    pl.semaphore_signal(barrier, inc=1, device_id={"tie": partner}, device_id_type=MESH)
    for k in range(1, pairs):
        pl.semaphore_signal(
            barrier, inc=1, device_id={"tie": member(k, parity)}, device_id_type=MESH
        )
    pl.semaphore_wait(barrier, pairs)

    order = [(k, q) for k in list(range(1, pairs)) + [0] for q in range(own)]
    first, second = {}, {}
    for k, q in order:
        slot = k * own + q
        first[k, q] = pltpu.make_async_remote_copy(
            src_ref=part.at[member(k, 1 - parity) * own + q],
            dst_ref=got.at[slot],
            send_sem=s1.at[slot],
            recv_sem=r1.at[slot],
            device_id={"tie": partner},
            device_id_type=MESH,
        )
        first[k, q].start()
    for k, q in order:
        slot = k * own + q
        first[k, q].wait_recv()
        mine = member(k, parity) * own + q
        if k == 0:
            out[q] = part[mine] + got[slot]
        else:
            summed[slot] = part[mine] + got[slot]
            second[k, q] = pltpu.make_async_remote_copy(
                src_ref=summed.at[slot],
                dst_ref=far.at[slot],
                send_sem=s2.at[slot],
                recv_sem=r2.at[slot],
                device_id={"tie": member(k, parity)},
                device_id_type=MESH,
            )
            second[k, q].start()
    for k, q in order:
        if k:
            second[k, q].wait_recv()
            out[q] += far[k * own + q]
    for k, q in order:
        first[k, q].wait_send()
        if k:
            second[k, q].wait_send()


def scatter_sum(partials, n):
    scenes, high, wide = partials.shape
    own = scenes // n
    slots = own * (n // 2)
    block = (slots, high, wide)
    dma = pltpu.SemaphoreType.DMA((slots,))
    return pl.pallas_call(
        functools.partial(scatter_kernel, n, own),
        out_shape=jax.ShapeDtypeStruct((own, high, wide), F32),
        in_specs=[VMEM],
        out_specs=VMEM,
        scratch_shapes=[pltpu.VMEM(block, F32)] * 3 + [dma] * 4,
        compiler_params=pltpu.CompilerParams(collective_id=0, has_side_effects=True),
        name="scatter",
    )(partials)


def three_parts(x):
    high = x.astype(BF16)
    rest = x - high.astype(F32)
    middle = rest.astype(BF16)
    return high, middle, (rest - middle.astype(F32)).astype(BF16)


def eliminate(panels, first_column):
    shape = panels[0].shape
    row_index = lax.broadcasted_iota(jnp.int32, shape, 0)
    lane = lax.broadcasted_iota(jnp.int32, shape, 1)
    for j in range(shape[0]):
        c = first_column + j
        for q, panel in enumerate(panels):
            column = jnp.broadcast_to(panel[:, c : c + 1], shape)
            scaled = panel[j : j + 1] / column[j : j + 1]
            panels[q] = panel - jnp.where(row_index > j, column, 0.0) * scaled
    above = lane >= row_index + first_column
    on_diagonal = lane == row_index + first_column
    done = []
    for panel in panels:
        diagonal = jnp.sum(jnp.where(on_diagonal, panel, 0.0), 1, keepdims=True)
        root = jnp.broadcast_to(jnp.sqrt(diagonal), shape)
        done.append(jnp.where(above, panel / root, 0.0))
    return done


def factor_kernel(damping, merged, sens, out, reduced, info):
    own, width, _ = info.shape
    spline = out.shape[1]
    half = width // 2
    row_index = lax.broadcasted_iota(jnp.int32, (width, width), 0)
    lane = lax.broadcasted_iota(jnp.int32, (width, width), 1)
    on_diagonal = (row_index == lane) & (row_index < spline)
    for q in range(own):
        side = merged[q, half : 2 * half]
        top = jnp.concatenate([merged[q, :half], side], 1)
        bottom = jnp.concatenate([side.T, merged[q, 2 * half :]], 1)
        whole = jnp.concatenate([top, bottom], 0)
        s = sens[q]
        mixed = whole
        for piece in three_parts(whole):
            mixed = mixed + jnp.dot(piece, s, preferred_element_type=F32)
        result = mixed + over_rows(s.astype(F32), mixed, HIGHEST)
        info[q] = result + jnp.where(on_diagonal, damping[q], 0.0)
    for start in range(0, spline, PANEL):
        base = start // LANES * LANES
        panels = [info[q, start : start + PANEL, base:] for q in range(own)]
        rows = eliminate(panels, start - base)
        for q in range(own):
            out[q, start : start + PANEL, base:] = rows[q]
        if base:
            out[:, start : start + PANEL, :base] = jnp.zeros((own, PANEL, base), F32)
        after = start + PANEL
        left = after // LANES * LANES
        for q in range(own):
            rest = rows[q][:, left - base :]
            info[q, after:, left:] -= over_rows(rest, rest, HIGHEST)[after - left :]
    total = info[0, spline:, half:]
    for q in range(1, own):
        total = total + info[q, spline:, half:]
    total = total[:, spline - half :]
    middle = (width - spline) // 2
    reduced[...] = jnp.concatenate([total[:middle], total[middle:]], 1)


def factor_scenes(merged, sensitivity, damping, width):
    own = damping.shape[0]
    spline = sensitivity.shape[1]
    half = width // 2
    mine = lax.dynamic_slice_in_dim(sensitivity, lax.axis_index("tie") * own, own)
    beyond = width - spline
    mine = jnp.pad(mine, ((0, 0), (0, beyond), (0, beyond)))
    return pl.pallas_call(
        factor_kernel,
        in_specs=[pl.BlockSpec(memory_space=pltpu.SMEM), VMEM, VMEM],
        out_specs=[VMEM, VMEM],
        scratch_shapes=[pltpu.VMEM((own, width, width), F32)],
        out_shape=[
            jax.ShapeDtypeStruct((own, spline, width), F32),
            jax.ShapeDtypeStruct(((width - spline) // 2, 2 * (width - spline)), F32),
        ],
        name="factor",
    )(damping, merged, mine)


def total_kernel(axes, x, out, *scratch):
    barrier = pltpu.get_barrier_semaphore()
    for name, n in axes:
        me = lax.axis_index(name)
        for k in range(1, n):
            pl.semaphore_signal(
                barrier, inc=1, device_id={name: lax.rem(me + k, n)}, device_id_type=MESH
            )
    pl.semaphore_wait(barrier, sum(n - 1 for _, n in axes))
    value = x
    for at, (name, n) in enumerate(axes):
        slots, send, recv = scratch[3 * at : 3 * at + 3]
        me = lax.axis_index(name)
        slots[0] = value[...]
        copies = []
        for k in range(1, n):
            copies.append(
                pltpu.make_async_remote_copy(
                    src_ref=slots.at[0],
                    dst_ref=slots.at[k],
                    send_sem=send.at[k],
                    recv_sem=recv.at[k],
                    device_id={name: lax.rem(me + k, n)},
                    device_id_type=MESH,
                )
            )
            copies[-1].start()
        for copy in copies:
            copy.wait_recv()
        acc = slots[me]
        for i in range(1, n):
            acc = acc + slots[lax.rem(me - i + n, n)]
        for copy in copies:
            copy.wait_send()
        out[...] = acc
        value = out


def total_sum(x, axes):
    scratch = []
    for _, n in axes:
        scratch += [pltpu.VMEM((n,) + x.shape, F32)]
        scratch += [pltpu.SemaphoreType.DMA((n,))] * 2
    return pl.pallas_call(
        functools.partial(total_kernel, axes),
        out_shape=jax.ShapeDtypeStruct(x.shape, F32),
        in_specs=[VMEM],
        out_specs=VMEM,
        scratch_shapes=scratch,
        compiler_params=pltpu.CompilerParams(collective_id=1, has_side_effects=True),
        name="total",
    )(x)


def last_kernel(scale, x, prior, out):
    shared = prior.shape[0]
    lane = lax.broadcasted_iota(jnp.int32, (shared, shared), 1)
    row = lax.broadcasted_iota(jnp.int32, (shared, shared), 0)
    packed = x[...]
    value = jnp.concatenate([packed[:, :shared], packed[:, shared:]], 0)
    value = value * scale + jnp.where(lane == row, prior[...], 0.0)
    out[...] = eliminate([value], 0)[0]


def last_factor(x, prior, scale):
    shared = prior.shape[0]
    return pl.pallas_call(
        functools.partial(last_kernel, scale),
        out_shape=jax.ShapeDtypeStruct((shared, shared), F32),
        in_specs=[VMEM, VMEM],
        out_specs=VMEM,
        name="last",
    )(x, prior[:, None])


def on_device(axes, tie_rows, point_counts, pattern, sensitivity, damping, prior):
    sizes = dict(axes)
    width = tie_rows.shape[2]
    partials = merged_partials(tie_rows, point_counts, pattern)
    merged = scatter_sum(partials, sizes["tie"])
    scene_rows, reduced = factor_scenes(merged, sensitivity, damping, width)
    total = total_sum(reduced, axes)
    scenes = damping.shape[0] * math.prod(sizes.values())
    return scene_rows, last_factor(total, prior, 1.0 / scenes)


def solution(mesh):
    axes = (("tie", mesh.shape["tie"]), ("scene", mesh.shape["scene"]))
    placed = (
        P("tie", None, None),
        P("tie"),
        P("scene", "tie"),
        P("scene", None, None),
        P(("scene", "tie")),
        P(),
    )
    return jax.shard_map(
        functools.partial(on_device, axes),
        mesh=mesh,
        in_specs=placed,
        out_specs=(P(("scene", "tie"), None, None), P()),
        check_vma=False,
    )
```

profile of v0, /device:TPU:0, one launch (start us, length us, event | category | flops | bytes accessed | tf_op | source)
XLA Modules:
  0.0 89.3 jit_solution(2293691526619693867)
XLA Ops:
  0.6 0.0 copy-start
  0.7 1.3 %convert_reduce_fusion = (s32[96]{0:T(128)}, pred[16,96]{1,0:T(8,128)(4,1)S(1)}) fusion(s32[16,96]{1,0:T(8,128)} %param.8), kind=kLoop, calls=%fused_computation.4 | loop fusion | flops 4512 | bytes 8064 | tf_op jit(solution)/shard_map/reduce_sum | solution.py:75
  2.0 0.1 multiply_reduce_fusion
  2.2 0.1 copy.14
  2.3 0.7 reshape.25.order
  3.0 15.7 %grams.1.part = f32[16,384,128]{2,1,0:T(8,128)} custom-call(s32[96]{0:T(128)} %counts.1, s32[1536]{0:T(1024)} %reshape.25.order, s32[96]{0:T(128)} %get-tuple-element.6.active, bf16[96,256,256]{2,1,0:T(8,128)(2,1)} %rows_ref.1), custom_call_target="tpu_custom_call" | custom-call | tf_op jit(solution)/shard_map/grams/pallas_call | solution.py:64
  18.6 0.0 copy-start.1
  18.6 25.3 %scatter.1.merged = f32[4,384,128]{2,1,0:T(8,128)} custom-call(f32[16,384,128]{2,1,0:T(8,128)} %grams.1.part), custom_call_target="tpu_custom_call" | custom-call | tf_op jit(solution)/shard_map/scatter/pallas_call | solution.py:142
  44.0 0.0 copy-done
  44.0 0.9 pad.4.sens
  44.9 24.2 %factor.1 = (f32[4,192,256]{2,1,0:T(8,128)}, f32[32,128]{1,0:T(8,128)}) custom-call(f32[4]{0:T(128)} %damping.1, f32[4,384,128]{2,1,0:T(8,128)} %scatter.1.merged, bf16[4,256,256]{2,1,0:T(8,128)(2,1)} %pad.4.sens), custom_call_target="tpu_custom_call" | custom-call | tf_op jit(solution)/shard_map/factor/pallas_call | solution.py:226
  69.0 12.7 %total.1.x = f32[32,128]{1,0:T(8,128)} custom-call(f32[32,128]{1,0:T(8,128)} %get-tuple-element.5.x), custom_call_target="tpu_custom_call" | custom-call | tf_op jit(solution)/shard_map/total/pallas_call | solution.py:282
  81.7 0.0 copy-done.1
  81.7 0.7 copy.15.prior
  82.4 6.9 %last.1 = f32[64,64]{1,0:T(8,128)} custom-call(f32[32,128]{1,0:T(8,128)} %total.1.x, f32[64,1]{1,0:T(8,128)} %copy.15.prior), custom_call_target="tpu_custom_call" | custom-call | tf_op jit(solution)/shard_map/last/pallas_call | solution.py:305
  (5 shorter events, 0.1 us)
Async XLA Ops:
  0.6 43.3 %copy-start = (bf16[16,192,192]{2,1,0:T(8,128)(2,1)S(1)}, bf16[16,192,192]{2,1,0:T(8,128)(2,1)}, u32[]{:S(2)}) copy-start(bf16[16,192,192]{2,1,0:T(8,128)(2,1)} %param.9) | copy-start | bytes 3538948
  18.6 63.1 %copy-start.1 = (f32[64]{0:T(128)S(1)}, f32[64]{0:T(128)}, u32[]{:S(2)}) copy-start(f32[64]{0:T(128)} %param.11) | copy-start | bytes 772
where the time goes:
time: 89.9 us; the launch traced here: 89.3 us
  Pallas kernels  84.7 us (94%)
  local copies, waits for them, and re-layouts  2.37 us (3%)
  other arithmetic  1.5 us (2%)
    pallas_call x1, Pallas kernels, scatter_sum(): pl.pallas_call(functools.partial(scatter_kernel, n, own), out_shape=jax.S...  25.3 us
    pallas_call x1, Pallas kernels, factor_scenes(): pl.pallas_call(factor_kernel, in_specs=[pl.BlockSpec(memory_space=pltpu.S...  24.2 us
    pallas_call x1, Pallas kernels, merged_partials(): pl.pallas_call(functools.partial(gram_kernel, chunk, scenes), grid_spec=p...  15.7 us
    pallas_call x1, Pallas kernels, total_sum(): pl.pallas_call(functools.partial(total_kernel, axes), out_shape=jax.Shape...  12.7 us
    pallas_call x1, Pallas kernels, last_factor(): pl.pallas_call(functools.partial(last_kernel, scale), out_shape=jax.Shape...  6.86 us

commit v1 on v0

--- a/solution.py
+++ b/solution.py
@@ -9,18 +9,16 @@
 from jax.sharding import PartitionSpec as P
 
 MESH = pl.DeviceIdType.MESH
-HIGHEST = lax.Precision.HIGHEST
 F32 = jnp.float32
 BF16 = jnp.bfloat16
 PANEL = 32
 LANES = 128
+SUB = 8
 VMEM = pl.BlockSpec(memory_space=pltpu.VMEM)
 
 
-def over_rows(a, b, precision=None):
-    return lax.dot_general(
-        a, b, (((0,), (0,)), ((), ())), precision=precision, preferred_element_type=F32
-    )
+def over_rows(a, b):
+    return lax.dot_general(a, b, (((0,), (0,)), ((), ())), preferred_element_type=F32)
 
 
 def gram_kernel(chunk, most, counts, order, active, rows_ref, out_ref, gram_ref):
@@ -150,37 +148,55 @@
     )(partials)
 
 
-def three_parts(x):
+def two_parts(x):
     high = x.astype(BF16)
-    rest = x - high.astype(F32)
-    middle = rest.astype(BF16)
-    return high, middle, (rest - middle.astype(F32)).astype(BF16)
-
-
-def eliminate(panels, first_column):
-    shape = panels[0].shape
-    row_index = lax.broadcasted_iota(jnp.int32, shape, 0)
-    lane = lax.broadcasted_iota(jnp.int32, shape, 1)
-    for j in range(shape[0]):
-        c = first_column + j
-        for q, panel in enumerate(panels):
-            column = jnp.broadcast_to(panel[:, c : c + 1], shape)
-            scaled = panel[j : j + 1] / column[j : j + 1]
-            panels[q] = panel - jnp.where(row_index > j, column, 0.0) * scaled
-    above = lane >= row_index + first_column
-    on_diagonal = lane == row_index + first_column
-    done = []
-    for panel in panels:
-        diagonal = jnp.sum(jnp.where(on_diagonal, panel, 0.0), 1, keepdims=True)
-        root = jnp.broadcast_to(jnp.sqrt(diagonal), shape)
-        done.append(jnp.where(above, panel / root, 0.0))
-    return done
-
-
-def factor_kernel(damping, merged, sens, out, reduced, info):
+    return high, (x - high.astype(F32)).astype(BF16)
+
+def eliminate(panels, first):
+    height, wide = panels[0].shape
+    tile = (SUB, LANES)
+    count = height // SUB
+    rows = [[p[SUB * h : SUB * (h + 1)] for h in range(count)] for p in panels]
+    row_index = lax.broadcasted_iota(jnp.int32, (SUB, wide), 0)
+    lane = lax.broadcasted_iota(jnp.int32, (SUB, wide), 1)
+    tile_row = lax.broadcasted_iota(jnp.int32, tile, 0)
+    below = [tile_row > k for k in range(SUB)]
+    def spread(x):
+        return x if wide == LANES else (jnp.concatenate([x] * (wide // LANES), 1) if wide > LANES else x[:, :wide])
+    for g in range(count):
+        start = first + SUB * g
+        cols = [
+            [[jnp.broadcast_to(r[h][:, start + m : start + m + 1], tile) for h in range(g, count)] for m in range(SUB)]
+            for r in rows
+        ]
+        for q, r in enumerate(rows):
+            b = cols[q]
+            pivots = b[0][0]
+            for k in range(SUB):
+                inverse = 1.0 / b[k][0][k : k + 1]
+                pivots = jnp.where(tile_row == k, b[k][0], pivots)
+                scaled = r[g][k : k + 1] * spread(inverse)
+                factors = [b[m][0][k : k + 1] * inverse for m in range(k + 1, SUB)]
+                for h in range(g, count):
+                    column = b[k][h - g]
+                    if h == g:
+                        if k == SUB - 1:
+                            continue
+                        column = jnp.where(below[k], column, 0.0)
+                    for m in range(k + 1, SUB):
+                        b[m][h - g] = b[m][h - g] - column * factors[m - k - 1]
+                    r[h] = r[h] - spread(column) * scaled
+            r[g] = jnp.where(lane >= row_index + start, r[g] * spread(lax.rsqrt(pivots)), 0.0)
+    return rows
+
+def factor_kernel(panel, damping, merged, sens, out, reduced, info, spread_sens):
     own, width, _ = info.shape
     spline = out.shape[1]
     half = width // 2
+    beyond = width - spline
+    for q in range(own):
+        wide = jnp.concatenate([sens[q], jnp.zeros((spline, beyond), BF16)], 1)
+        spread_sens[q] = jnp.concatenate([wide, jnp.zeros((beyond, width), BF16)], 0)
     row_index = lax.broadcasted_iota(jnp.int32, (width, width), 0)
     lane = lax.broadcasted_iota(jnp.int32, (width, width), 1)
     on_diagonal = (row_index == lane) & (row_index < spline)
@@ -189,25 +205,29 @@
         top = jnp.concatenate([merged[q, :half], side], 1)
         bottom = jnp.concatenate([side.T, merged[q, 2 * half :]], 1)
         whole = jnp.concatenate([top, bottom], 0)
-        s = sens[q]
-        mixed = whole
-        for piece in three_parts(whole):
-            mixed = mixed + jnp.dot(piece, s, preferred_element_type=F32)
-        result = mixed + over_rows(s.astype(F32), mixed, HIGHEST)
+        s = spread_sens[q]
+        mixed = whole + sum(
+            jnp.dot(piece, s, preferred_element_type=F32) for piece in two_parts(whole)
+        )
+        result = mixed + sum(over_rows(s, piece) for piece in two_parts(mixed))
         info[q] = result + jnp.where(on_diagonal, damping[q], 0.0)
-    for start in range(0, spline, PANEL):
+    for start in range(0, spline, panel):
         base = start // LANES * LANES
-        panels = [info[q, start : start + PANEL, base:] for q in range(own)]
+        panels = [info[q, start : start + panel, base:] for q in range(own)]
         rows = eliminate(panels, start - base)
+        if base:
+            out[:, start : start + panel, :base] = jnp.zeros((own, panel, base), F32)
+        after = start + panel
         for q in range(own):
-            out[q, start : start + PANEL, base:] = rows[q]
-        if base:
-            out[:, start : start + PANEL, :base] = jnp.zeros((own, PANEL, base), F32)
-        after = start + PANEL
-        left = after // LANES * LANES
-        for q in range(own):
-            rest = rows[q][:, left - base :]
-            info[q, after:, left:] -= over_rows(rest, rest, HIGHEST)[after - left :]
+            block = jnp.concatenate(rows[q], 0)
+            out[q, start : start + panel, base:] = block
+            high, low = two_parts(block)
+            left = jnp.concatenate([high, high, low], 0)
+            right = jnp.concatenate([high, low, high], 0)
+            for top in range(after // LANES * LANES, width, LANES):
+                skip = max(after - top, 0)
+                update = over_rows(left[:, top - base : top - base + LANES], right[:, top - base :])
+                info[q, top + skip : top + LANES, top:] -= update[skip:]
     total = info[0, spline:, half:]
     for q in range(1, own):
         total = total + info[q, spline:, half:]
@@ -215,22 +235,22 @@
     middle = (width - spline) // 2
     reduced[...] = jnp.concatenate([total[:middle], total[middle:]], 1)
 
-
 def factor_scenes(merged, sensitivity, damping, width):
     own = damping.shape[0]
     spline = sensitivity.shape[1]
-    half = width // 2
+    beyond = width - spline
     mine = lax.dynamic_slice_in_dim(sensitivity, lax.axis_index("tie") * own, own)
-    beyond = width - spline
-    mine = jnp.pad(mine, ((0, 0), (0, beyond), (0, beyond)))
-    return pl.pallas_call(
-        factor_kernel,
+    return pl.pallas_call(
+        functools.partial(factor_kernel, PANEL),
         in_specs=[pl.BlockSpec(memory_space=pltpu.SMEM), VMEM, VMEM],
         out_specs=[VMEM, VMEM],
-        scratch_shapes=[pltpu.VMEM((own, width, width), F32)],
+        scratch_shapes=[
+            pltpu.VMEM((own, width, width), F32),
+            pltpu.VMEM((own, width, width), BF16),
+        ],
         out_shape=[
             jax.ShapeDtypeStruct((own, spline, width), F32),
-            jax.ShapeDtypeStruct(((width - spline) // 2, 2 * (width - spline)), F32),
+            jax.ShapeDtypeStruct((beyond // 2, 2 * beyond), F32),
         ],
         name="factor",
     )(damping, merged, mine)
@@ -291,14 +311,13 @@
 
 
 def last_kernel(scale, x, prior, out):
-    shared = prior.shape[0]
+    shared = prior.shape[1]
     lane = lax.broadcasted_iota(jnp.int32, (shared, shared), 1)
     row = lax.broadcasted_iota(jnp.int32, (shared, shared), 0)
     packed = x[...]
     value = jnp.concatenate([packed[:, :shared], packed[:, shared:]], 0)
     value = value * scale + jnp.where(lane == row, prior[...], 0.0)
-    out[...] = eliminate([value], 0)[0]
-
+    out[...] = jnp.concatenate(eliminate([value], 0)[0], 0)
 
 def last_factor(x, prior, scale):
     shared = prior.shape[0]
@@ -308,7 +327,7 @@
         in_specs=[VMEM, VMEM],
         out_specs=VMEM,
         name="last",
-    )(x, prior[:, None])
+    )(x, prior[None, :])
 
 
 def on_device(axes, tie_rows, point_counts, pattern, sensitivity, damping, prior):

time: 89.9 us -> 70.9 us (0.79)
  Pallas kernels: 84.7 us -> 66.6 us
    pallas_call x1, Pallas kernels: 24.2 us -> 9.68 us  [factor_scenes(): pl.pallas_call(functools.partial(factor_kernel, PANEL), in_specs=[pl.Bloc...]
    pallas_call x1, Pallas kernels: 6.86 us -> 2.81 us  [last_factor(): pl.pallas_call(functools.partial(last_kernel, scale), out_shape=jax.Shape...]
where the time goes in v1:
time: 70.9 us; the launch traced here: 70.3 us
  Pallas kernels  66.6 us (94%)
  local copies, waits for them, and re-layouts  1.55 us (2%)
  other arithmetic  1.5 us (2%)
    pallas_call x1, Pallas kernels, scatter_sum(): pl.pallas_call(functools.partial(scatter_kernel, n, own), out_shape=jax.S...  25.3 us
    pallas_call x1, Pallas kernels, merged_partials(): pl.pallas_call(functools.partial(gram_kernel, chunk, scenes), grid_spec=p...  15.5 us
    pallas_call x1, Pallas kernels, total_sum(): pl.pallas_call(functools.partial(total_kernel, axes), out_shape=jax.Shape...  13.3 us
    pallas_call x1, Pallas kernels, factor_scenes(): pl.pallas_call(functools.partial(factor_kernel, PANEL), in_specs=[pl.Bloc...  9.68 us
    pallas_call x1, Pallas kernels, last_factor(): pl.pallas_call(functools.partial(last_kernel, scale), out_shape=jax.Shape...  2.81 us

profile of v1, /device:TPU:0, one launch (start us, length us, event | category | flops | bytes accessed | tf_op | source)
XLA Modules:
  0.0 70.3 jit_solution(13828987630049169975)
XLA Ops:
  0.6 0.0 copy-start
  0.7 1.3 %convert_reduce_fusion = (s32[96]{0:T(128)}, pred[16,96]{1,0:T(8,128)(4,1)S(1)}) fusion(s32[16,96]{1,0:T(8,128)} %param.8), kind=kLoop, calls=%fused_computation.4 | loop fusion | flops 4512 | bytes 8064 | tf_op jit(solution)/shard_map/reduce_sum | solution.py:73
  2.0 0.1 multiply_reduce_fusion
  2.2 0.1 copy.12
  2.3 0.7 reshape.25.order
  3.0 15.5 %grams.1.part = f32[16,384,128]{2,1,0:T(8,128)} custom-call(s32[96]{0:T(128)} %counts.1, s32[1536]{0:T(1024)} %reshape.25.order, s32[96]{0:T(128)} %get-tuple-element.6.active, bf16[96,256,256]{2,1,0:T(8,128)(2,1)} %rows_ref.1), custom_call_target="tpu_custom_call" | custom-call | tf_op jit(solution)/shard_map/grams/pallas_call | solution.py:62
  18.5 25.3 %scatter.1.merged = f32[4,384,128]{2,1,0:T(8,128)} custom-call(f32[16,384,128]{2,1,0:T(8,128)} %grams.1.part), custom_call_target="tpu_custom_call" | custom-call | tf_op jit(solution)/shard_map/scatter/pallas_call | solution.py:140
  43.7 0.0 copy-done
  43.7 0.8 %constant_dynamic-slice_fusion.sens = bf16[4,192,192]{2,1,0:T(8,128)(2,1)} fusion(bf16[16,192,192]{2,1,0:T(8,128)(2,1)S(1)} %copy-done, s32[]{:T(128)S(6)} %select_n.8), kind=kLoop, calls=%fused_computation.10 | loop fusion | bytes 589828 | tf_op jit(solution)/shard_map/dynamic_slice | solution.py:242
  44.5 9.7 %factor.1 = (f32[4,192,256]{2,1,0:T(8,128)}, f32[32,128]{1,0:T(8,128)}) custom-call(f32[4]{0:T(128)} %damping.1, f32[4,384,128]{2,1,0:T(8,128)} %scatter.1.merged, bf16[4,192,192]{2,1,0:T(8,128)(2,1)} %constant_dynamic-slice_fusion.sens), custom_call_target="tpu_custom_call" | custom-call | tf_op jit(solution)/shard_map/factor/pallas_call | solution.py:243
  54.2 13.3 %total.1.x = f32[32,128]{1,0:T(8,128)} custom-call(f32[32,128]{1,0:T(8,128)} %get-tuple-element.5.x), custom_call_target="tpu_custom_call" | custom-call | tf_op jit(solution)/shard_map/total/pallas_call | solution.py:302
  67.5 2.8 %last.1 = f32[64,64]{1,0:T(8,128)} custom-call(f32[32,128]{1,0:T(8,128)} %total.1.x, f32[1,64]{1,0:T(1,128)} %bitcast.5), custom_call_target="tpu_custom_call" | custom-call | tf_op jit(solution)/shard_map/last/pallas_call | solution.py:324
  (4 shorter events, 0.1 us)
Async XLA Ops:
  0.6 43.1 %copy-start = (bf16[16,192,192]{2,1,0:T(8,128)(2,1)S(1)}, bf16[16,192,192]{2,1,0:T(8,128)(2,1)}, u32[]{:S(2)}) copy-start(bf16[16,192,192]{2,1,0:T(8,128)(2,1)} %param.9) | copy-start | bytes 3538948

commit v2 on v1

v2 whole, which is shorter than its diff:
```python
import functools
import math

import jax
import jax.numpy as jnp
from jax import lax
from jax.experimental import pallas as pl
from jax.experimental.pallas import tpu as pltpu
from jax.sharding import PartitionSpec as P


MESH = pl.DeviceIdType.MESH
F32 = jnp.float32
BF16 = jnp.bfloat16
PANEL = 32
LANES = 128
SUB = 8
UNROLL = 8
DEPTH = 32
PIECES = 2
VMEM = pl.BlockSpec(memory_space=pltpu.VMEM)


def over_rows(a, b):
    return lax.dot_general(a, b, (((0,), (0,)), ((), ())), preferred_element_type=F32)


def gram_kernel(groups, own, pairs, counts, pattern, rows, *rest):
    outs = rest[: len(groups)]
    ring, acc, entries, arrived = rest[len(groups) :]
    depth, _, wide = ring.shape
    half = wide // 2
    total = pattern.shape[1]
    stride = 1 << (total - 1).bit_length()
    me = lax.axis_index("tie")

    def fetch(n):
        at = lax.rem(n, depth)
        block = entries[n] & (stride - 1)
        return pltpu.make_async_copy(rows.at[block], ring.at[at], arrived.at[at])

    def start_fetch(n, carry):
        fetch(n).start()
        return carry

    filled = jnp.int32(0)
    place = 0
    for hop, side, offset, size in groups:
        device = lax.rem(me // 2 + hop, pairs) * 2 + lax.rem(me + side, 2)

        def scan(q, n, device=device, offset=offset, place=place):
            scene = device * own + offset + q
            base = (place + q) * stride
            was = n
            for block in range(total):
                entries[n] = base + block
                n = n + pattern[scene, block]
            lax.fori_loop(jnp.minimum(was, depth), jnp.minimum(n, depth), start_fetch, 0)
            return n

        filled = lax.fori_loop(0, size, scan, filled)
        place += size
    acc[...] = jnp.zeros_like(acc)
    reach = lax.broadcasted_iota(jnp.int32, (2 * SUB, wide), 1)

    def step(it, carry):
        for u in range(UNROLL):
            n = it * UNROLL + u

            @pl.when(n < filled)
            def _(n=n):
                fetch(n).wait()

        for u in range(UNROLL):
            n = it * UNROLL + u
            at = jnp.minimum(n, filled - 1)
            entry = entries[at]
            keep = jnp.where(n < filled, 2 * counts[entry & (stride - 1)], 0)
            value = ring[lax.rem(at, depth)]
            mask = jnp.where(reach < keep, 1.0, 0.0).astype(BF16)
            kept = value.T * jnp.concatenate([mask] * (wide // (2 * SUB)), 0)
            top = jnp.dot(kept[:half], value, preferred_element_type=F32)
            bottom = jnp.dot(kept[half:], value[:, half:], preferred_element_type=F32)
            to = entry // stride
            acc[to, :half] += top[:, :half]
            acc[to, half : 2 * half] += top[:, half:]
            acc[to, 2 * half :] += bottom
        for u in range(UNROLL):
            n = it * UNROLL + u + depth

            @pl.when(n < filled)
            def _(n=n):
                fetch(n).start()

        return carry

    lax.fori_loop(0, (filled + UNROLL - 1) // UNROLL, step, 0)
    row = lax.broadcasted_iota(jnp.int32, (half, half), 0)
    lane = lax.broadcasted_iota(jnp.int32, (half, half), 1)
    first = lax.broadcasted_iota(jnp.int32, (SUB, half), 0) == 0
    place = 0
    for out, (_, _, _, size) in zip(outs, groups):
        for q in range(size):
            low = acc[place, 2 * half :]
            out[q, :half] = acc[place, half : 2 * half]
            out[q, half : 2 * half] = jnp.where(row <= lane, acc[place, :half], low)
            diagonal = jnp.sum(jnp.where(row == lane, low, 0.0), 0, keepdims=True)
            out[q, 2 * half :] = jnp.where(first, diagonal, 0.0)
            place += 1


def gram_sums(tie_rows, point_counts, pattern, groups, own, n):
    total, height, wide = tie_rows.shape
    half = wide // 2
    sizes = [group[3] for group in groups]
    most = sum(sizes)
    smem = pl.BlockSpec(memory_space=pltpu.SMEM)
    return pl.pallas_call(
        functools.partial(gram_kernel, groups, own, n // 2),
        in_specs=[smem, smem, pl.BlockSpec(memory_space=pl.ANY)],
        out_specs=[VMEM] * len(sizes),
        out_shape=[jax.ShapeDtypeStruct((size, wide + SUB, half), F32) for size in sizes],
        scratch_shapes=[
            pltpu.VMEM((DEPTH, height, wide), BF16),
            pltpu.VMEM((most, 3 * half, half), F32),
            pltpu.SMEM((most * total + 1,), jnp.int32),
            pltpu.SemaphoreType.DMA((DEPTH,)),
        ],
        compiler_params=pltpu.CompilerParams(vmem_limit_bytes=56 << 20),
    )(point_counts, pattern, tie_rows)


def swap_cores(x, n):
    return lax.ppermute(x, "tie", [(t, t ^ 1) for t in range(n)])


def send_over(x, n, hop):
    pairs = n // 2
    return lax.ppermute(x, "tie", [(t, (t // 2 + hop) % pairs * 2 + t % 2) for t in range(n)])


def merged_sums(tie_rows, point_counts, pattern, own, n):
    size = own // PIECES
    parts = []
    for hop in range(1, n // 2):
        for offset in range(0, own, size):
            groups = [(hop, side, offset, size) for side in (1, 0)]
            theirs, mine = gram_sums(tie_rows, point_counts, pattern, groups, own, n)
            both = mine + swap_cores(theirs, n)
            both, point_counts = lax.optimization_barrier((both, point_counts))
            parts.append((offset, send_over(both, n, hop)))
    groups = [(0, 1, 0, own), (0, 0, 0, own)]
    theirs, mine = gram_sums(tie_rows, point_counts, pattern, groups, own, n)
    return [(0, mine), (0, swap_cores(theirs, n))] + parts


def two_parts(x):
    high = x.astype(BF16)
    return high, (x - high.astype(F32)).astype(BF16)


def eliminate(panels, first):
    height, wide = panels[0].shape
    tile = (SUB, LANES)
    count = height // SUB
    rows = [[p[SUB * h : SUB * (h + 1)] for h in range(count)] for p in panels]
    row_index = lax.broadcasted_iota(jnp.int32, (SUB, wide), 0)
    lane = lax.broadcasted_iota(jnp.int32, (SUB, wide), 1)
    tile_row = lax.broadcasted_iota(jnp.int32, tile, 0)
    below = [tile_row > k for k in range(SUB)]

    def spread(x):
        return x if wide == LANES else (jnp.concatenate([x] * (wide // LANES), 1) if wide > LANES else x[:, :wide])

    for g in range(count):
        start = first + SUB * g
        cols = [
            [[jnp.broadcast_to(r[h][:, start + m : start + m + 1], tile) for h in range(g, count)] for m in range(SUB)]
            for r in rows
        ]
        for q, r in enumerate(rows):
            b = cols[q]
            pivots = b[0][0]
            for k in range(SUB):
                inverse = 1.0 / b[k][0][k : k + 1]
                pivots = jnp.where(tile_row == k, b[k][0], pivots)
                scaled = r[g][k : k + 1] * spread(inverse)
                factors = [b[m][0][k : k + 1] * inverse for m in range(k + 1, SUB)]
                for h in range(g, count):
                    column = b[k][h - g]
                    if h == g:
                        if k == SUB - 1:
                            continue
                        column = jnp.where(below[k], column, 0.0)
                    for m in range(k + 1, SUB):
                        b[m][h - g] = b[m][h - g] - column * factors[m - k - 1]
                    r[h] = r[h] - spread(column) * scaled
            r[g] = jnp.where(lane >= row_index + start, r[g] * spread(lax.rsqrt(pivots)), 0.0)
    return rows


def factor_kernel(panel, offsets, damping, sens, *rest):
    parts = rest[: len(offsets)]
    out, reduced, info, spread_sens = rest[len(offsets) :]
    own, width, _ = info.shape
    spline = out.shape[1]
    half = width // 2
    beyond = width - spline
    for q in range(own):
        wide = jnp.concatenate([sens[q], jnp.zeros((spline, beyond), BF16)], 1)
        spread_sens[q] = jnp.concatenate([wide, jnp.zeros((beyond, width), BF16)], 0)
    row_index = lax.broadcasted_iota(jnp.int32, (width, width), 0)
    lane = lax.broadcasted_iota(jnp.int32, (width, width), 1)
    on_diagonal = (row_index == lane) & (row_index < spline)
    across = lane[:half, :half] - row_index[:half, :half]
    for q in range(own):
        packed = sum(
            part[q - offset]
            for offset, part in zip(offsets, parts)
            if offset <= q < offset + part.shape[0]
        )
        side, both = packed[:half], packed[half : 2 * half]
        upper = jnp.where(across > 0, both, 0.0)
        first = jnp.where(across >= 0, both, upper.T)
        lower = jnp.where(across < 0, both, 0.0)
        last = lower + jnp.where(across == 0, packed[2 * half : 2 * half + 1], lower.T)
        top = jnp.concatenate([first, side], 1)
        bottom = jnp.concatenate([side.T, last], 1)
        whole = jnp.concatenate([top, bottom], 0)
        s = spread_sens[q]
        mixed = whole + sum(
            jnp.dot(piece, s, preferred_element_type=F32) for piece in two_parts(whole)
        )
        result = mixed + sum(over_rows(s, piece) for piece in two_parts(mixed))
        info[q] = result + jnp.where(on_diagonal, damping[q], 0.0)
    for start in range(0, spline, panel):
        base = start // LANES * LANES
        panels = [info[q, start : start + panel, base:] for q in range(own)]
        rows = eliminate(panels, start - base)
        if base:
            out[:, start : start + panel, :base] = jnp.zeros((own, panel, base), F32)
        after = start + panel
        for q in range(own):
            block = jnp.concatenate(rows[q], 0)
            out[q, start : start + panel, base:] = block
            high, low = two_parts(block)
            left = jnp.concatenate([high, high, low], 0)
            right = jnp.concatenate([high, low, high], 0)
            for top in range(after // LANES * LANES, width, LANES):
                skip = max(after - top, 0)
                update = over_rows(left[:, top - base : top - base + LANES], right[:, top - base :])
                info[q, top + skip : top + LANES, top:] -= update[skip:]
    total = info[0, spline:, half:]
    for q in range(1, own):
        total = total + info[q, spline:, half:]
    total = total[:, spline - half :]
    middle = (width - spline) // 2
    reduced[...] = jnp.concatenate([total[:middle], total[middle:]], 1)


def factor_scenes(parts, sensitivity, damping, width):
    own = damping.shape[0]
    spline = sensitivity.shape[1]
    beyond = width - spline
    mine = lax.dynamic_slice_in_dim(sensitivity, lax.axis_index("tie") * own, own)
    offsets = [offset for offset, _ in parts]
    return pl.pallas_call(
        functools.partial(factor_kernel, PANEL, offsets),
        in_specs=[pl.BlockSpec(memory_space=pltpu.SMEM)] + [VMEM] * (1 + len(parts)),
        out_specs=[VMEM, VMEM],
        scratch_shapes=[
            pltpu.VMEM((own, width, width), F32),
            pltpu.VMEM((own, width, width), BF16),
        ],
        out_shape=[
            jax.ShapeDtypeStruct((own, spline, width), F32),
            jax.ShapeDtypeStruct((beyond // 2, 2 * beyond), F32),
        ],
        compiler_params=pltpu.CompilerParams(vmem_limit_bytes=32 << 20),
        name="factor",
    )(damping, mine, *(part for _, part in parts))


def total_kernel(axes, x, out, *scratch):
    barrier = pltpu.get_barrier_semaphore()
    for name, n in axes:
        me = lax.axis_index(name)
        for k in range(1, n):
            pl.semaphore_signal(
                barrier, inc=1, device_id={name: lax.rem(me + k, n)}, device_id_type=MESH
            )
    pl.semaphore_wait(barrier, sum(n - 1 for _, n in axes))
    value = x
    for at, (name, n) in enumerate(axes):
        slots, send, recv = scratch[3 * at : 3 * at + 3]
        me = lax.axis_index(name)
        slots[0] = value[...]
        copies = []
        for k in range(1, n):
            copies.append(
                pltpu.make_async_remote_copy(
                    src_ref=slots.at[0],
                    dst_ref=slots.at[k],
                    send_sem=send.at[k],
                    recv_sem=recv.at[k],
                    device_id={name: lax.rem(me + k, n)},
                    device_id_type=MESH,
                )
            )
            copies[-1].start()
        for copy in copies:
            copy.wait_recv()
        acc = slots[me]
        for i in range(1, n):
            acc = acc + slots[lax.rem(me - i + n, n)]
        for copy in copies:
            copy.wait_send()
        out[...] = acc
        value = out


def total_sum(x, axes):
    scratch = []
    for _, n in axes:
        scratch += [pltpu.VMEM((n,) + x.shape, F32)]
        scratch += [pltpu.SemaphoreType.DMA((n,))] * 2
    return pl.pallas_call(
        functools.partial(total_kernel, axes),
        out_shape=jax.ShapeDtypeStruct(x.shape, F32),
        in_specs=[VMEM],
        out_specs=VMEM,
        scratch_shapes=scratch,
        compiler_params=pltpu.CompilerParams(collective_id=1, has_side_effects=True),
        name="total",
    )(x)


def last_kernel(scale, x, prior, out):
    shared = prior.shape[1]
    lane = lax.broadcasted_iota(jnp.int32, (shared, shared), 1)
    row = lax.broadcasted_iota(jnp.int32, (shared, shared), 0)
    packed = x[...]
    value = jnp.concatenate([packed[:, :shared], packed[:, shared:]], 0)
    value = value * scale + jnp.where(lane == row, prior[...], 0.0)
    out[...] = jnp.concatenate(eliminate([value], 0)[0], 0)


def last_factor(x, prior, scale):
    shared = prior.shape[0]
    return pl.pallas_call(
        functools.partial(last_kernel, scale),
        out_shape=jax.ShapeDtypeStruct((shared, shared), F32),
        in_specs=[VMEM, VMEM],
        out_specs=VMEM,
        name="last",
    )(x, prior[None, :])


def on_device(axes, tie_rows, point_counts, pattern, sensitivity, damping, prior):
    sizes = dict(axes)
    own = damping.shape[0]
    width = tie_rows.shape[2]
    parts = merged_sums(tie_rows, point_counts, pattern, own, sizes["tie"])
    scene_rows, reduced = factor_scenes(parts, sensitivity, damping, width)
    total = total_sum(reduced, axes)
    scenes = own * math.prod(sizes.values())
    return scene_rows, last_factor(total, prior, 1.0 / scenes)


def solution(mesh):
    axes = (("tie", mesh.shape["tie"]), ("scene", mesh.shape["scene"]))
    placed = (
        P("tie", None, None),
        P("tie"),
        P("scene", "tie"),
        P("scene", None, None),
        P(("scene", "tie")),
        P(),
    )
    return jax.shard_map(
        functools.partial(on_device, axes),
        mesh=mesh,
        in_specs=placed,
        out_specs=(P(("scene", "tie"), None, None), P()),
        check_vma=False,
    )
```

time: 70.9 us -> 69 us (0.973)
  Pallas kernels: 66.6 us -> 43.8 us
  waiting for transfers between devices: 0 us -> 15.5 us
  starting transfers between devices: 0 us -> 4.84 us
    pallas_call x3 -> x4, Pallas kernels: 50.4 us -> 26.4 us  [the longest x3 17.4 us: gram_sums(): pl.pallas_call(functools.partial(gram_kernel, groups, own, n // 2), in_sp...]
    ppermute x0 -> x5, waiting for transfers between devices: none -> 15.5 us  [the longest x2 12.8 us: send_over(): lax.ppermute(x, 'tie', [(t, (t // 2 + hop) % pairs * 2 + t % 2) for t in...]
    ppermute x0 -> x5, starting transfers between devices: none -> 4.84 us  [the longest x2 2.43 us: send_over(): lax.ppermute(x, 'tie', [(t, (t // 2 + hop) % pairs * 2 + t % 2) for t in...]
    add x0 -> x2, other arithmetic: none -> 1.96 us  [merged_sums(): both = mine + swap_cores(theirs, n)]
    unnamed x2 -> x8, local copies, waits for them, and re-layouts: 0.01 us -> 1.67 us
    reduce_sum x3 -> x0, other arithmetic: 1.49 us -> none  [the longest x1 1.34 us: merged_partials(): jnp.sum(seen, 1)]
    pallas_call x1, Pallas kernels: 13.3 us -> 14.5 us  [total_sum(): pl.pallas_call(functools.partial(total_kernel, axes), out_shape=jax.Shape...]
    dynamic_slice x1, local copies, waits for them, and re-layouts: 0.77 us -> 0.03 us  [factor_scenes(): lax.dynamic_slice_in_dim(sensitivity, lax.axis_index('tie') * own, own)]
  transfers between devices with their start and end apart: 0 -> 5, of which waited for: 0 -> 4; matrix products, arithmetic and copies ran while one was open for 0% -> 0% of each run, Pallas kernels for 0% -> 0%
where the time goes in v2:
time: 69 us; the launch traced here: 68.5 us
  Pallas kernels  43.8 us (63%)
  waiting for transfers between devices  15.5 us (22%)
  starting transfers between devices  4.84 us (7%)
  other arithmetic  1.96 us (3%)
  local copies, waits for them, and re-layouts  1.69 us (2%)
  between operations  0.7 us (1%)
    pallas_call x3, Pallas kernels, gram_sums(): pl.pallas_call(functools.partial(gram_kernel, groups, own, n // 2), in_sp...  17.4 us
    pallas_call x1, Pallas kernels, total_sum(): pl.pallas_call(functools.partial(total_kernel, axes), out_shape=jax.Shape...  14.5 us
    ppermute x2, waiting for transfers between devices, send_over(): lax.ppermute(x, 'tie', [(t, (t // 2 + hop) % pairs * 2 + t % 2) for t in...  12.8 us
    pallas_call x1, Pallas kernels, factor_scenes(): pl.pallas_call(functools.partial(factor_kernel, PANEL, offsets), in_specs...  9.03 us
    pallas_call x1, Pallas kernels, last_factor(): pl.pallas_call(functools.partial(last_kernel, scale), out_shape=jax.Shape...  2.81 us
    ppermute x3, waiting for transfers between devices, swap_cores(): return lax.ppermute(x, 'tie', [(t, t ^ 1) for t in range(n)])  2.77 us
    ppermute x2, starting transfers between devices, send_over(): lax.ppermute(x, 'tie', [(t, (t // 2 + hop) % pairs * 2 + t % 2) for t in...  2.43 us
    ppermute x3, starting transfers between devices, swap_cores(): return lax.ppermute(x, 'tie', [(t, t ^ 1) for t in range(n)])  2.41 us
  transfers between devices with their start and end apart: 5, of which 4 were waited for; matrix products, arithmetic and copies ran while one was open for 0% of the time, Pallas kernels for 0%

profile of v2, /device:TPU:0, one launch (start us, length us, event | category | flops | bytes accessed | tf_op | source)
XLA Modules:
  0.0 68.5 jit_solution(16384574616219667023)
XLA Ops:
  0.6 0.0 copy-start
  0.6 5.1 %shard_map.77 = (f32[2,264,128]{2,1,0:T(8,128)}, f32[2,264,128]{2,1,0:T(8,128)}) custom-call(s32[96]{0:T(128)} %counts.3, s32[16,96]{1,0:T(8,128)} %pattern.5, bf16[96,256,256]{2,1,0:T(8,128)(2,1)} %rows.5), custom_call_target="tpu_custom_call" | custom-call | tf_op jit(solution)/shard_map/pallas_call | solution.py:118
  5.8 1.1 %collective-permute-start = (f32[2,264,128]{2,1,0:T(8,128)}, f32[2,264,128]{2,1,0:T(8,128)S(1)}, u32[]{:S(2)}, u32[]{:S(2)}) collective-permute-start(f32[2,264,128]{2,1,0:T(8,128)} %get-tuple-element.15), channel_id=1, source_target_pairs={{0,1},{1,0},{2,3},{3,2},{4,5},{5,4},{6,7},{7,6},{8,9},{9,8},{10,11... | collective-permute-start | bytes 811016 | tf_op jit(solution)/shard_map/ppermute | solution.py:134
  6.9 1.4 %collective-permute-done = f32[2,264,128]{2,1,0:T(8,128)S(1)} collective-permute-done((f32[2,264,128]{2,1,0:T(8,128)}, f32[2,264,128]{2,1,0:T(8,128)S(1)}, u32[]{:S(2)}, u32[]{:S(2)}) %collective-permute-start) | collective-permute-done | bytes 270368 | tf_op jit(solution)/shard_map/ppermute | solution.py:134
  8.3 1.0 %add.10 = f32[2,264,128]{2,1,0:T(8,128)S(1)} add(f32[2,264,128]{2,1,0:T(8,128)} %get-tuple-element.14, f32[2,264,128]{2,1,0:T(8,128)S(1)} %collective-permute-done) | non-fusion elementwise | flops 67584 | bytes 811008 | tf_op jit(solution)/shard_map/add | solution.py:149
  9.2 5.0 %shard_map.78 = (f32[2,264,128]{2,1,0:T(8,128)}, f32[2,264,128]{2,1,0:T(8,128)}) custom-call(s32[96]{0:T(128)} %counts.3, s32[16,96]{1,0:T(8,128)} %pattern.5, bf16[96,256,256]{2,1,0:T(8,128)(2,1)} %rows.5), custom_call_target="tpu_custom_call" | custom-call | tf_op jit(solution)/shard_map/pallas_call | solution.py:118
  14.3 0.9 %collective-permute-start.1 = (f32[2,264,128]{2,1,0:T(8,128)}, f32[2,264,128]{2,1,0:T(8,128)S(1)}, u32[]{:S(2)}, u32[]{:S(2)}) collective-permute-start(f32[2,264,128]{2,1,0:T(8,128)} %get-tuple-element.18), channel_id=1, source_target_pairs={{0,1},{1,0},{2,3},{3,2},{4,5},{5,4},{6,7},{7,6},{8,9},{9,8},{10,11... | collective-permute-start | bytes 811016 | tf_op jit(solution)/shard_map/ppermute | solution.py:134
  15.1 1.4 %collective-permute-done.1 = f32[2,264,128]{2,1,0:T(8,128)S(1)} collective-permute-done((f32[2,264,128]{2,1,0:T(8,128)}, f32[2,264,128]{2,1,0:T(8,128)S(1)}, u32[]{:S(2)}, u32[]{:S(2)}) %collective-permute-start.1) | collective-permute-done | bytes 270368 | tf_op jit(solution)/shard_map/ppermute | solution.py:134
  16.5 1.0 %add.11 = f32[2,264,128]{2,1,0:T(8,128)S(1)} add(f32[2,264,128]{2,1,0:T(8,128)} %get-tuple-element.17, f32[2,264,128]{2,1,0:T(8,128)S(1)} %collective-permute-done.1) | non-fusion elementwise | flops 67584 | bytes 811008 | tf_op jit(solution)/shard_map/add | solution.py:149
  17.5 0.0 copy-start.3
  17.5 7.3 %shard_map.79 = (f32[4,264,128]{2,1,0:T(8,128)}, f32[4,264,128]{2,1,0:T(8,128)}) custom-call(s32[96]{0:T(128)} %counts.3, s32[16,96]{1,0:T(8,128)} %pattern.5, bf16[96,256,256]{2,1,0:T(8,128)(2,1)} %rows.5), custom_call_target="tpu_custom_call" | custom-call | tf_op jit(solution)/shard_map/pallas_call | solution.py:118
  24.8 0.4 collective-permute-start.2
  25.2 2.4 %collective-permute-start.3 = (f32[2,264,128]{2,1,0:T(8,128)S(1)}, f32[2,264,128]{2,1,0:T(8,128)S(1)}, u32[]{:S(2)}, u32[]{:S(2)}) collective-permute-start(f32[2,264,128]{2,1,0:T(8,128)S(1)} %add.10), channel_id=1, source_target_pairs={{0,2},{1,3},{2,0},{3,1},{4,6},{5,7},{6,4},{7,5},{8,10},{9,11},{10,... | collective-permute-start | bytes 811016 | tf_op jit(solution)/shard_map/ppermute | solution.py:139
  27.6 0.1 collective-permute-start.4
  27.7 0.0 copy-done
  27.7 7.2 %collective-permute-done.3.rest_2_ = f32[2,264,128]{2,1,0:T(8,128)S(1)} collective-permute-done((f32[2,264,128]{2,1,0:T(8,128)S(1)}, f32[2,264,128]{2,1,0:T(8,128)S(1)}, u32[]{:S(2)}, u32[]{:S(2)}) %collective-permute-start.3) | collective-permute-done | bytes 270368 | tf_op jit(solution)/shard_map/ppermute | solution.py:139
  34.9 5.5 %collective-permute-done.4.rest_3_ = f32[2,264,128]{2,1,0:T(8,128)S(1)} collective-permute-done((f32[2,264,128]{2,1,0:T(8,128)S(1)}, f32[2,264,128]{2,1,0:T(8,128)S(1)}, u32[]{:S(2)}, u32[]{:S(2)}) %collective-permute-start.4) | collective-permute-done | bytes 270368 | tf_op jit(solution)/shard_map/ppermute | solution.py:139
  40.4 0.0 collective-permute-done.2.rest_1_
  40.4 0.0 copy-done.3
  40.5 1.0 %copy-done.1 = f32[4,264,128]{2,1,0:T(8,128)S(1)} copy-done((f32[4,264,128]{2,1,0:T(8,128)S(1)}, f32[4,264,128]{2,1,0:T(8,128)}, u32[]{:S(2)}) %copy-start.1) | copy-done | bytes 540696
  41.5 9.0 %factor.1 = (f32[4,192,256]{2,1,0:T(8,128)}, f32[32,128]{1,0:T(8,128)S(1)}) custom-call(f32[4]{0:T(128)S(1)} %copy-done.3, bf16[4,192,192]{2,1,0:T(8,128)(2,1)S(1)} %constant_dynamic-slice_fusion.sens, f32[4,264,128]{2,1,0:T(8,128)S(1)} %copy-done.1, f32[4,264,128]{2,1,0:T(8,128)S(1)} %collective-permute-done.2.rest_1_, ...), custom_call_target="tpu_custom_call" | custom-call | tf_op jit(solution)/shard_map/factor/pallas_call | solution.py:267
  50.5 0.6 copy-done.2
  51.1 14.5 %total.1.x = f32[32,128]{1,0:T(8,128)} custom-call(f32[32,128]{1,0:T(8,128)} %copy-done.2), custom_call_target="tpu_custom_call" | custom-call | tf_op jit(solution)/shard_map/total/pallas_call | solution.py:327
  65.7 2.8 %last.1 = f32[64,64]{1,0:T(8,128)} custom-call(f32[32,128]{1,0:T(8,128)} %total.1.x, f32[1,64]{1,0:T(1,128)} %bitcast.1), custom_call_target="tpu_custom_call" | custom-call | tf_op jit(solution)/shard_map/last/pallas_call | solution.py:350
  (3 shorter events, 0.0 us)
Async XLA Ops:
  0.6 27.0 %copy-start = (bf16[16,192,192]{2,1,0:T(8,128)(2,1)S(1)}, bf16[16,192,192]{2,1,0:T(8,128)(2,1)}, u32[]{:S(2)}) copy-start(bf16[16,192,192]{2,1,0:T(8,128)(2,1)} %param.9) | copy-start | bytes 3538948
  5.8 2.5 %collective-permute-start = (f32[2,264,128]{2,1,0:T(8,128)}, f32[2,264,128]{2,1,0:T(8,128)S(1)}, u32[]{:S(2)}, u32[]{:S(2)}) collective-permute-start(f32[2,264,128]{2,1,0:T(8,128)} %get-tuple-element.15), channel_id=1, source_target_pairs={{0,1},{1,0},{2,3},{3,2},{4,5},{5,4},{6,7},{7,6},{8,9},{9,8},{10,11... | collective-permute-start | bytes 811016 | tf_op jit(solution)/shard_map/ppermute | solution.py:134
  14.3 2.2 %collective-permute-start.1 = (f32[2,264,128]{2,1,0:T(8,128)}, f32[2,264,128]{2,1,0:T(8,128)S(1)}, u32[]{:S(2)}, u32[]{:S(2)}) collective-permute-start(f32[2,264,128]{2,1,0:T(8,128)} %get-tuple-element.18), channel_id=1, source_target_pairs={{0,1},{1,0},{2,3},{3,2},{4,5},{5,4},{6,7},{7,6},{8,9},{9,8},{10,11... | collective-permute-start | bytes 811016 | tf_op jit(solution)/shard_map/ppermute | solution.py:134
  17.5 22.9 %copy-start.3 = (f32[4]{0:T(128)S(1)}, f32[4]{0:T(128)}, u32[]{:S(2)}) copy-start(f32[4]{0:T(128)} %damping.1) | copy-start | bytes 52
  24.8 15.7 %collective-permute-start.2 = (f32[4,264,128]{2,1,0:T(8,128)}, f32[4,264,128]{2,1,0:T(8,128)S(1)}, u32[]{:S(2)}, u32[]{:S(2)}) collective-permute-start(f32[4,264,128]{2,1,0:T(8,128)} %get-tuple-element.21), channel_id=1, source_target_pairs={{0,1},{1,0},{2,3},{3,2},{4,5},{5,4},{6,7},{7,6},{8,9},{9,8},{10,11... | collective-permute-start | bytes 1622024 | tf_op jit(solution)/shard_map/ppermute | solution.py:134
  25.2 9.7 %collective-permute-start.3 = (f32[2,264,128]{2,1,0:T(8,128)S(1)}, f32[2,264,128]{2,1,0:T(8,128)S(1)}, u32[]{:S(2)}, u32[]{:S(2)}) collective-permute-start(f32[2,264,128]{2,1,0:T(8,128)S(1)} %add.10), channel_id=1, source_target_pairs={{0,2},{1,3},{2,0},{3,1},{4,6},{5,7},{6,4},{7,5},{8,10},{9,11},{10,... | collective-permute-start | bytes 811016 | tf_op jit(solution)/shard_map/ppermute | solution.py:139
  27.6 12.9 %collective-permute-start.4 = (f32[2,264,128]{2,1,0:T(8,128)S(1)}, f32[2,264,128]{2,1,0:T(8,128)S(1)}, u32[]{:S(2)}, u32[]{:S(2)}) collective-permute-start(f32[2,264,128]{2,1,0:T(8,128)S(1)} %add.11), channel_id=1, source_target_pairs={{0,2},{1,3},{2,0},{3,1},{4,6},{5,7},{6,4},{7,5},{8,10},{9,11},{10,... | collective-permute-start | bytes 811016 | tf_op jit(solution)/shard_map/ppermute | solution.py:139
  40.5 1.0 %copy-start.1 = (f32[4,264,128]{2,1,0:T(8,128)S(1)}, f32[4,264,128]{2,1,0:T(8,128)}, u32[]{:S(2)}) copy-start(f32[4,264,128]{2,1,0:T(8,128)} %get-tuple-element.20.rest_0_) | copy-start | bytes 1622020
  50.5 0.6 copy-start.2

commit v3 on v2

--- a/solution.py
+++ b/solution.py
@@ -1,5 +1,4 @@
 import functools
-import math
 
 import jax
 import jax.numpy as jnp
@@ -17,7 +16,7 @@
 SUB = 8
 UNROLL = 8
 DEPTH = 32
-PIECES = 2
+PIECES = 1
 VMEM = pl.BlockSpec(memory_space=pltpu.VMEM)
 
 
@@ -126,7 +125,7 @@
             pltpu.SMEM((most * total + 1,), jnp.int32),
             pltpu.SemaphoreType.DMA((DEPTH,)),
         ],
-        compiler_params=pltpu.CompilerParams(vmem_limit_bytes=56 << 20),
+        compiler_params=pltpu.CompilerParams(vmem_limit_bytes=50 << 20),
     )(point_counts, pattern, tie_rows)
 
 
@@ -199,9 +198,89 @@
     return rows
 
 
-def factor_kernel(panel, offsets, damping, sens, *rest):
+def exchange(ref, slots, send, recv, name, n, width=None):
+    me = lax.axis_index(name)
+    copies = []
+    for k in range(1, n):
+        other = lax.rem(me + k, n)
+        part = ref if width is None else ref.at[pl.ds(pl.multiple_of(other * width, width), width)]
+        copies.append(
+            pltpu.make_async_remote_copy(
+                src_ref=part,
+                dst_ref=slots.at[k],
+                send_sem=send.at[k],
+                recv_sem=recv.at[k],
+                device_id={name: other},
+                device_id_type=MESH,
+            )
+        )
+        copies[-1].start()
+    return copies
+
+
+def added(slots, name, n):
+    me = lax.axis_index(name)
+    acc = slots[me]
+    for i in range(1, n):
+        acc = acc + slots[lax.rem(me - i + n, n)]
+    return acc
+
+
+def finish_kernel(panel, offsets, axes, scale, damping, sens, prior, *rest):
     parts = rest[: len(offsets)]
-    out, reduced, info, spread_sens = rest[len(offsets) :]
+    scene_rows, factor, info, spread_sens, out = rest[len(offsets) : len(offsets) + 5]
+    mine, near, wide_slots, whole, written, s1, r1, s2, r2, s3, r3 = rest[len(offsets) + 5 :]
+    barrier = pltpu.get_barrier_semaphore()
+    for name, n in axes:
+        me = lax.axis_index(name)
+        for k in range(1, n):
+            pl.semaphore_signal(
+                barrier, inc=1, device_id={name: lax.rem(me + k, n)}, device_id_type=MESH
+            )
+    mine[...] = factor_scenes(panel, offsets, damping, sens, parts, out, info, spread_sens)
+    rows = pltpu.make_async_copy(out, scene_rows, written)
+    rows.start()
+    pl.semaphore_wait(barrier, sum(n - 1 for _, n in axes))
+    (tie, n), (scene, groups) = axes
+    chunk = mine.shape[0] // n
+    me = lax.axis_index(tie)
+    own = pl.ds(pl.multiple_of(me * chunk, chunk), chunk)
+    near[0] = mine[own]
+    first = exchange(mine, near, s1, r1, tie, n, chunk)
+    for copy in first:
+        copy.wait_recv()
+    wide_slots[0] = added(near, tie, n)
+    second = exchange(wide_slots.at[0], wide_slots, s2, r2, scene, groups)
+    for copy in second:
+        copy.wait_recv()
+    whole[own] = added(wide_slots, scene, groups)
+    third = []
+    for k in range(1, n):
+        third.append(
+            pltpu.make_async_remote_copy(
+                src_ref=whole.at[own],
+                dst_ref=whole.at[own],
+                send_sem=s3.at[k],
+                recv_sem=r3.at[k],
+                device_id={tie: lax.rem(me + k, n)},
+                device_id_type=MESH,
+            )
+        )
+        third[-1].start()
+    for copy in third:
+        copy.wait_recv()
+    shared = factor.shape[0]
+    lane = lax.broadcasted_iota(jnp.int32, (shared, shared), 1)
+    row = lax.broadcasted_iota(jnp.int32, (shared, shared), 0)
+    value = jnp.concatenate([whole[:, :shared], whole[:, shared:]], 0)
+    value = value * scale + jnp.where(lane == row, prior[...], 0.0)
+    factor[...] = jnp.concatenate(eliminate([value], 0)[0], 0)
+    for copy in first + second + third:
+        copy.wait_send()
+    rows.wait()
+
+
+def factor_scenes(panel, offsets, damping, sens, parts, out, info, spread_sens):
     own, width, _ = info.shape
     spline = out.shape[1]
     half = width // 2
@@ -255,105 +334,48 @@
         total = total + info[q, spline:, half:]
     total = total[:, spline - half :]
     middle = (width - spline) // 2
-    reduced[...] = jnp.concatenate([total[:middle], total[middle:]], 1)
-
-
-def factor_scenes(parts, sensitivity, damping, width):
+    return jnp.concatenate([total[:middle], total[middle:]], 1)
+
+
+def finish(parts, sensitivity, damping, prior, width, axes):
     own = damping.shape[0]
     spline = sensitivity.shape[1]
     beyond = width - spline
+    (_, n), (_, groups) = axes
     mine = lax.dynamic_slice_in_dim(sensitivity, lax.axis_index("tie") * own, own)
     offsets = [offset for offset, _ in parts]
+    scale = 1.0 / (own * n * groups)
+    block = (beyond // 2 // n, 2 * beyond)
+    dma = pltpu.SemaphoreType.DMA
     return pl.pallas_call(
-        functools.partial(factor_kernel, PANEL, offsets),
-        in_specs=[pl.BlockSpec(memory_space=pltpu.SMEM)] + [VMEM] * (1 + len(parts)),
-        out_specs=[VMEM, VMEM],
+        functools.partial(finish_kernel, PANEL, offsets, axes, scale),
+        in_specs=[pl.BlockSpec(memory_space=pltpu.SMEM)] + [VMEM] * (2 + len(parts)),
+        out_specs=[pl.BlockSpec(memory_space=pl.ANY), VMEM],
         scratch_shapes=[
             pltpu.VMEM((own, width, width), F32),
             pltpu.VMEM((own, width, width), BF16),
+            pltpu.VMEM((own, spline, width), F32),
+            pltpu.VMEM((beyond // 2, 2 * beyond), F32),
+            pltpu.VMEM((n,) + block, F32),
+            pltpu.VMEM((groups,) + block, F32),
+            pltpu.VMEM((beyond // 2, 2 * beyond), F32),
+            dma,
+            dma((n,)),
+            dma((n,)),
+            dma((groups,)),
+            dma((groups,)),
+            dma((n,)),
+            dma((n,)),
         ],
         out_shape=[
             jax.ShapeDtypeStruct((own, spline, width), F32),
-            jax.ShapeDtypeStruct((beyond // 2, 2 * beyond), F32),
+            jax.ShapeDtypeStruct((beyond, beyond), F32),
         ],
-        compiler_params=pltpu.CompilerParams(vmem_limit_bytes=32 << 20),
-        name="factor",
-    )(damping, mine, *(part for _, part in parts))
-
-
-def total_kernel(axes, x, out, *scratch):
-    barrier = pltpu.get_barrier_semaphore()
-    for name, n in axes:
-        me = lax.axis_index(name)
-        for k in range(1, n):
-            pl.semaphore_signal(
-                barrier, inc=1, device_id={name: lax.rem(me + k, n)}, device_id_type=MESH
-            )
-    pl.semaphore_wait(barrier, sum(n - 1 for _, n in axes))
-    value = x
-    for at, (name, n) in enumerate(axes):
-        slots, send, recv = scratch[3 * at : 3 * at + 3]
-        me = lax.axis_index(name)
-        slots[0] = value[...]
-        copies = []
-        for k in range(1, n):
-            copies.append(
-                pltpu.make_async_remote_copy(
-                    src_ref=slots.at[0],
-                    dst_ref=slots.at[k],
-                    send_sem=send.at[k],
-                    recv_sem=recv.at[k],
-                    device_id={name: lax.rem(me + k, n)},
-                    device_id_type=MESH,
-                )
-            )
-            copies[-1].start()
-        for copy in copies:
-            copy.wait_recv()
-        acc = slots[me]
-        for i in range(1, n):
-            acc = acc + slots[lax.rem(me - i + n, n)]
-        for copy in copies:
-            copy.wait_send()
-        out[...] = acc
-        value = out
-
-
-def total_sum(x, axes):
-    scratch = []
-    for _, n in axes:
-        scratch += [pltpu.VMEM((n,) + x.shape, F32)]
-        scratch += [pltpu.SemaphoreType.DMA((n,))] * 2
-    return pl.pallas_call(
-        functools.partial(total_kernel, axes),
-        out_shape=jax.ShapeDtypeStruct(x.shape, F32),
-        in_specs=[VMEM],
-        out_specs=VMEM,
-        scratch_shapes=scratch,
-        compiler_params=pltpu.CompilerParams(collective_id=1, has_side_effects=True),
-        name="total",
-    )(x)
-
-
-def last_kernel(scale, x, prior, out):
-    shared = prior.shape[1]
-    lane = lax.broadcasted_iota(jnp.int32, (shared, shared), 1)
-    row = lax.broadcasted_iota(jnp.int32, (shared, shared), 0)
-    packed = x[...]
-    value = jnp.concatenate([packed[:, :shared], packed[:, shared:]], 0)
-    value = value * scale + jnp.where(lane == row, prior[...], 0.0)
-    out[...] = jnp.concatenate(eliminate([value], 0)[0], 0)
-
-
-def last_factor(x, prior, scale):
-    shared = prior.shape[0]
-    return pl.pallas_call(
-        functools.partial(last_kernel, scale),
-        out_shape=jax.ShapeDtypeStruct((shared, shared), F32),
-        in_specs=[VMEM, VMEM],
-        out_specs=VMEM,
-        name="last",
-    )(x, prior[None, :])
+        compiler_params=pltpu.CompilerParams(
+            collective_id=0, has_side_effects=True, vmem_limit_bytes=32 << 20
+        ),
+        name="finish",
+    )(damping, mine, prior[None, :], *(part for _, part in parts))
 
 
 def on_device(axes, tie_rows, point_counts, pattern, sensitivity, damping, prior):
@@ -361,10 +383,7 @@
     own = damping.shape[0]
     width = tie_rows.shape[2]
     parts = merged_sums(tie_rows, point_counts, pattern, own, sizes["tie"])
-    scene_rows, reduced = factor_scenes(parts, sensitivity, damping, width)
-    total = total_sum(reduced, axes)
-    scenes = own * math.prod(sizes.values())
-    return scene_rows, last_factor(total, prior, 1.0 / scenes)
+    return finish(parts, sensitivity, damping, prior, width, axes)
 
 
 def solution(mesh):

time: 69 us -> 50.9 us (0.74)
  Pallas kernels: 43.8 us -> 33.7 us
  waiting for transfers between devices: 15.5 us -> 7.75 us
  local copies, waits for them, and re-layouts: 1.69 us -> 3 us
  other arithmetic: 1.96 us -> 0.85 us
    ppermute x2 -> x1, waiting for transfers between devices: 12.8 us -> 6.18 us  [send_over(): lax.ppermute(x, 'tie', [(t, (t // 2 + hop) % pairs * 2 + t % 2) for t in...]
    pallas_call x3 -> x2, Pallas kernels: 17.4 us -> 12 us  [gram_sums(): pl.pallas_call(functools.partial(gram_kernel, groups, own, n // 2), in_sp...]
    pallas_call x3 -> x1, Pallas kernels: 26.4 us -> 21.7 us  [finish(): pl.pallas_call(functools.partial(finish_kernel, PANEL, offsets, axes, sca...]
    unnamed x8 -> x12, local copies, waits for them, and re-layouts: 1.67 us -> 2.98 us
    ppermute x3 -> x2, waiting for transfers between devices: 2.77 us -> 1.56 us  [swap_cores(): return lax.ppermute(x, 'tie', [(t, t ^ 1) for t in range(n)])]
    add x2 -> x1, other arithmetic: 1.96 us -> 0.85 us  [merged_sums(): both = mine + swap_cores(theirs, n)]
    ppermute x3 -> x2, starting transfers between devices: 2.41 us -> 1.76 us  [swap_cores(): return lax.ppermute(x, 'tie', [(t, t ^ 1) for t in range(n)])]
    ppermute x2 -> x1, starting transfers between devices: 2.43 us -> 2.87 us  [send_over(): lax.ppermute(x, 'tie', [(t, (t // 2 + hop) % pairs * 2 + t % 2) for t in...]
  transfers between devices with their start and end apart: 5 -> 3, of which waited for: 4 -> 2; matrix products, arithmetic and copies ran while one was open for 0% -> 0% of each run, Pallas kernels for 0% -> 13%
where the time goes in v3:
time: 50.9 us; the launch traced here: 50.6 us
  Pallas kernels  33.7 us (66%)
  waiting for transfers between devices  7.75 us (15%)
  starting transfers between devices  4.63 us (9%)
  local copies, waits for them, and re-layouts  3 us (6%)
  other arithmetic  0.85 us (2%)
  between operations  0.68 us (1%)
    pallas_call x1, Pallas kernels, finish(): pl.pallas_call(functools.partial(finish_kernel, PANEL, offsets, axes, sca...  21.7 us
    pallas_call x2, Pallas kernels, gram_sums(): pl.pallas_call(functools.partial(gram_kernel, groups, own, n // 2), in_sp...  12 us
    ppermute x1, waiting for transfers between devices, send_over(): lax.ppermute(x, 'tie', [(t, (t // 2 + hop) % pairs * 2 + t % 2) for t in...  6.18 us
    unnamed x12, local copies, waits for them, and re-layouts  2.98 us
    ppermute x1, starting transfers between devices, send_over(): lax.ppermute(x, 'tie', [(t, (t // 2 + hop) % pairs * 2 + t % 2) for t in...  2.87 us
    ppermute x2, starting transfers between devices, swap_cores(): return lax.ppermute(x, 'tie', [(t, t ^ 1) for t in range(n)])  1.76 us
    ppermute x2, waiting for transfers between devices, swap_cores(): return lax.ppermute(x, 'tie', [(t, t ^ 1) for t in range(n)])  1.56 us
  transfers between devices with their start and end apart: 3, of which 2 were waited for; matrix products, arithmetic and copies ran while one was open for 0% of the time, Pallas kernels for 13%

profile of v3, /device:TPU:0, one launch (start us, length us, event | category | flops | bytes accessed | tf_op | source)
XLA Modules:
  0.0 50.6 jit_solution(2271301499447847059)
XLA Ops:
  0.6 0.0 copy-start
  0.6 0.0 copy-start.1
  0.7 0.8 %copy-done.1 = s32[16,96]{1,0:T(8,128)S(1)} copy-done((s32[16,96]{1,0:T(8,128)S(1)}, s32[16,96]{1,0:T(8,128)}, u32[]{:S(2)}) %copy-start.1) | copy-done | bytes 6168
  1.5 0.0 copy-start.2
  1.5 0.7 %copy-done.2 = s32[96]{0:T(128)S(1)} copy-done((s32[96]{0:T(128)S(1)}, s32[96]{0:T(128)}, u32[]{:S(2)}) %copy-start.2) | copy-done | bytes 408
  2.1 5.3 %shard_map.77 = (f32[4,264,128]{2,1,0:T(8,128)S(1)}, f32[4,264,128]{2,1,0:T(8,128)S(1)}) custom-call(s32[96]{0:T(128)S(1)} %copy-done.2, s32[16,96]{1,0:T(8,128)S(1)} %copy-done.1, bf16[96,256,256]{2,1,0:T(8,128)(2,1)} %rows.3), custom_call_target="tpu_custom_call" | custom-call | tf_op jit(solution)/shard_map/pallas_call | solution.py:117
  7.5 1.6 %collective-permute-start = (f32[4,264,128]{2,1,0:T(8,128)S(1)}, f32[4,264,128]{2,1,0:T(8,128)S(1)}, u32[]{:S(2)}, u32[]{:S(2)}) collective-permute-start(f32[4,264,128]{2,1,0:T(8,128)S(1)} %get-tuple-element.9), channel_id=1, source_target_pairs={{0,1},{1,0},{2,3},{3,2},{4,5},{5,4},{6,7},{7,6},{8,9},{9,8},{10,11... | collective-permute-start | bytes 1622024 | tf_op jit(solution)/shard_map/ppermute | solution.py:133
  9.1 1.6 %collective-permute-done = f32[4,264,128]{2,1,0:T(8,128)S(1)} collective-permute-done((f32[4,264,128]{2,1,0:T(8,128)S(1)}, f32[4,264,128]{2,1,0:T(8,128)S(1)}, u32[]{:S(2)}, u32[]{:S(2)}) %collective-permute-start) | collective-permute-done | bytes 540704 | tf_op jit(solution)/shard_map/ppermute | solution.py:133
  10.6 0.8 %add.7 = f32[4,264,128]{2,1,0:T(8,128)} add(f32[4,264,128]{2,1,0:T(8,128)S(1)} %get-tuple-element.8, f32[4,264,128]{2,1,0:T(8,128)S(1)} %collective-permute-done) | non-fusion elementwise | flops 135168 | bytes 1622016 | tf_op jit(solution)/shard_map/add | solution.py:148
  11.5 0.0 copy-start.3
  11.5 0.0 copy-start.4
  11.5 2.9 %collective-permute-start.2 = (f32[4,264,128]{2,1,0:T(8,128)}, f32[4,264,128]{2,1,0:T(8,128)S(1)}, u32[]{:S(2)}, u32[]{:S(2)}) collective-permute-start(f32[4,264,128]{2,1,0:T(8,128)} %add.7), channel_id=1, source_target_pairs={{0,2},{1,3},{2,0},{3,1},{4,6},{5,7},{6,4},{7,5},{8,10},{9,11},{10,... | collective-permute-start | bytes 1622024 | tf_op jit(solution)/shard_map/ppermute | solution.py:138
  14.4 6.6 %shard_map.78 = (f32[4,264,128]{2,1,0:T(8,128)}, f32[4,264,128]{2,1,0:T(8,128)S(1)}) custom-call(s32[96]{0:T(128)S(1)} %copy-done.2, s32[16,96]{1,0:T(8,128)S(1)} %copy-done.1, bf16[96,256,256]{2,1,0:T(8,128)(2,1)} %rows.3), custom_call_target="tpu_custom_call" | custom-call | tf_op jit(solution)/shard_map/pallas_call | solution.py:117
  21.0 0.1 collective-permute-start.1
  21.2 0.0 copy-done
  21.2 6.2 %collective-permute-done.2.rest_2_ = f32[4,264,128]{2,1,0:T(8,128)S(1)} collective-permute-done((f32[4,264,128]{2,1,0:T(8,128)}, f32[4,264,128]{2,1,0:T(8,128)S(1)}, u32[]{:S(2)}, u32[]{:S(2)}) %collective-permute-start.2) | collective-permute-done | bytes 540704 | tf_op jit(solution)/shard_map/ppermute | solution.py:138
  27.4 0.0 collective-permute-done.1.rest_1_
  27.4 0.0 copy-done.3
  27.4 0.0 copy-done.4
  27.4 21.7 %finish.1 = (f32[4,192,256]{2,1,0:T(8,128)S(1)}, f32[64,64]{1,0:T(8,128)S(1)}) custom-call(f32[4]{0:T(128)S(1)} %copy-done.3, bf16[4,192,192]{2,1,0:T(8,128)(2,1)S(1)} %constant_dynamic-slice_fusion.sens, f32[1,64]{1,0:T(1,128)S(1)} %bitcast.1, f32[4,264,128]{2,1,0:T(8,128)S(1)} %get-tuple-element.11.rest_0_, ...), custom_call_target="tpu_custom_call" | custom-call | tf_op jit(solution)/shard_map/finish/pallas_call | solution.py:350
  49.1 0.9 %copy.10 = f32[4,192,256]{2,1,0:T(8,128)} copy(f32[4,192,256]{2,1,0:T(8,128)S(1)} %get-tuple-element.16) | data formatting | bytes 1572864
  50.0 0.6 %copy.11 = f32[64,64]{1,0:T(8,128)} copy(f32[64,64]{1,0:T(8,128)S(1)} %get-tuple-element.17) | data formatting | bytes 32768
  (1 shorter events, 0.0 us)
Async XLA Ops:
  0.6 20.5 %copy-start = (bf16[16,192,192]{2,1,0:T(8,128)(2,1)S(1)}, bf16[16,192,192]{2,1,0:T(8,128)(2,1)}, u32[]{:S(2)}) copy-start(bf16[16,192,192]{2,1,0:T(8,128)(2,1)} %param.9) | copy-start | bytes 3538948
  0.6 0.8 %copy-start.1 = (s32[16,96]{1,0:T(8,128)S(1)}, s32[16,96]{1,0:T(8,128)}, u32[]{:S(2)}) copy-start(s32[16,96]{1,0:T(8,128)} %pattern.3) | copy-start | bytes 18436
  1.5 0.7 %copy-start.2 = (s32[96]{0:T(128)S(1)}, s32[96]{0:T(128)}, u32[]{:S(2)}) copy-start(s32[96]{0:T(128)} %counts.2) | copy-start | bytes 1156
  7.5 3.2 %collective-permute-start = (f32[4,264,128]{2,1,0:T(8,128)S(1)}, f32[4,264,128]{2,1,0:T(8,128)S(1)}, u32[]{:S(2)}, u32[]{:S(2)}) collective-permute-start(f32[4,264,128]{2,1,0:T(8,128)S(1)} %get-tuple-element.9), channel_id=1, source_target_pairs={{0,1},{1,0},{2,3},{3,2},{4,5},{5,4},{6,7},{7,6},{8,9},{9,8},{10,11... | collective-permute-start | bytes 1622024 | tf_op jit(solution)/shard_map/ppermute | solution.py:133
  11.5 15.9 %copy-start.3 = (f32[4]{0:T(128)S(1)}, f32[4]{0:T(128)}, u32[]{:S(2)}) copy-start(f32[4]{0:T(128)} %damping.1) | copy-start | bytes 52
  11.5 15.9 %copy-start.4 = (f32[64]{0:T(128)S(1)}, f32[64]{0:T(128)}, u32[]{:S(2)}) copy-start(f32[64]{0:T(128)} %param.11) | copy-start | bytes 772
  11.5 15.9 %collective-permute-start.2 = (f32[4,264,128]{2,1,0:T(8,128)}, f32[4,264,128]{2,1,0:T(8,128)S(1)}, u32[]{:S(2)}, u32[]{:S(2)}) collective-permute-start(f32[4,264,128]{2,1,0:T(8,128)} %add.7), channel_id=1, source_target_pairs={{0,2},{1,3},{2,0},{3,1},{4,6},{5,7},{6,4},{7,5},{8,10},{9,11},{10,... | collective-permute-start | bytes 1622024 | tf_op jit(solution)/shard_map/ppermute | solution.py:138
  21.0 6.4 %collective-permute-start.1 = (f32[4,264,128]{2,1,0:T(8,128)}, f32[4,264,128]{2,1,0:T(8,128)S(1)}, u32[]{:S(2)}, u32[]{:S(2)}) collective-permute-start(f32[4,264,128]{2,1,0:T(8,128)} %get-tuple-element.12), channel_id=1, source_target_pairs={{0,1},{1,0},{2,3},{3,2},{4,5},{5,4},{6,7},{7,6},{8,9},{9,8},{10,11... | collective-permute-start | bytes 1622024 | tf_op jit(solution)/shard_map/ppermute | solution.py:133

commit v4 on v3

--- a/solution.py
+++ b/solution.py
@@ -125,7 +125,7 @@
             pltpu.SMEM((most * total + 1,), jnp.int32),
             pltpu.SemaphoreType.DMA((DEPTH,)),
         ],
-        compiler_params=pltpu.CompilerParams(vmem_limit_bytes=50 << 20),
+        compiler_params=pltpu.CompilerParams(vmem_limit_bytes=16 << 20),
     )(point_counts, pattern, tie_rows)
 
 
@@ -141,6 +141,9 @@
 def merged_sums(tie_rows, point_counts, pattern, own, n):
     size = own // PIECES
     parts = []
+    tie_rows, point_counts, pattern = (
+        pltpu.with_memory_space_constraint(x, pltpu.HBM) for x in (tie_rows, point_counts, pattern)
+    )
     for hop in range(1, n // 2):
         for offset in range(0, own, size):
             groups = [(hop, side, offset, size) for side in (1, 0)]
@@ -181,19 +184,20 @@
             b = cols[q]
             pivots = b[0][0]
             for k in range(SUB):
-                inverse = 1.0 / b[k][0][k : k + 1]
-                pivots = jnp.where(tile_row == k, b[k][0], pivots)
-                scaled = r[g][k : k + 1] * spread(inverse)
-                factors = [b[m][0][k : k + 1] * inverse for m in range(k + 1, SUB)]
+                pivot = jnp.broadcast_to(b[k][0][k : k + 1], tile)
+                inverse = 1.0 / pivot
+                pivots = jnp.where(tile_row == k, pivot, pivots)
+                row = jnp.broadcast_to(r[g][k : k + 1], (SUB, wide))
+                ahead = [jnp.broadcast_to(b[m][0][k : k + 1], tile) for m in range(k + 1, SUB)]
                 for h in range(g, count):
-                    column = b[k][h - g]
+                    column = b[k][h - g] * inverse
                     if h == g:
                         if k == SUB - 1:
                             continue
                         column = jnp.where(below[k], column, 0.0)
                     for m in range(k + 1, SUB):
-                        b[m][h - g] = b[m][h - g] - column * factors[m - k - 1]
-                    r[h] = r[h] - spread(column) * scaled
+                        b[m][h - g] = b[m][h - g] - column * ahead[m - k - 1]
+                    r[h] = r[h] - spread(column) * row
             r[g] = jnp.where(lane >= row_index + start, r[g] * spread(lax.rsqrt(pivots)), 0.0)
     return rows
 
@@ -378,12 +382,36 @@
     )(damping, mine, prior[None, :], *(part for _, part in parts))
 
 
+def emit_kernel(rows, factor, rows_out, factor_out, sems):
+    copies = [
+        pltpu.make_async_copy(rows, rows_out, sems.at[0]),
+        pltpu.make_async_copy(factor, factor_out, sems.at[1]),
+    ]
+    for copy in copies:
+        copy.start()
+    for copy in copies:
+        copy.wait()
+
+
+def emit(scene_rows, factor):
+    anywhere = pl.BlockSpec(memory_space=pl.ANY)
+    return pl.pallas_call(
+        emit_kernel,
+        in_specs=[anywhere] * 2,
+        out_specs=[anywhere] * 2,
+        scratch_shapes=[pltpu.SemaphoreType.DMA((2,))],
+        out_shape=[jax.ShapeDtypeStruct(x.shape, x.dtype) for x in (scene_rows, factor)],
+        compiler_params=pltpu.CompilerParams(vmem_limit_bytes=1 << 20),
+        name="emit",
+    )(scene_rows, factor)
+
+
 def on_device(axes, tie_rows, point_counts, pattern, sensitivity, damping, prior):
     sizes = dict(axes)
     own = damping.shape[0]
     width = tie_rows.shape[2]
     parts = merged_sums(tie_rows, point_counts, pattern, own, sizes["tie"])
-    return finish(parts, sensitivity, damping, prior, width, axes)
+    return emit(*finish(parts, sensitivity, damping, prior, width, axes))
 
 
 def solution(mesh):

time: 50.9 us -> 50.5 us (level)
  local copies, waits for them, and re-layouts: 3 us -> 0.04 us
  Pallas kernels: 33.7 us -> 36.4 us
    unnamed x12 -> x6, local copies, waits for them, and re-layouts: 2.98 us -> 0.02 us
    pallas_call x1, Pallas kernels: 21.7 us -> 23.2 us  [finish(): pl.pallas_call(functools.partial(finish_kernel, PANEL, offsets, axes, sca...]
    pallas_call x0 -> x1, Pallas kernels: none -> 0.9 us  [emit(): pl.pallas_call(emit_kernel, in_specs=[anywhere] * 2, out_specs=[anywhere]...]
where the time goes in v4:
time: 50.5 us; the launch traced here: 50.3 us
  Pallas kernels  36.4 us (72%)
  waiting for transfers between devices  7.62 us (15%)
  starting transfers between devices  4.63 us (9%)
  other arithmetic  0.86 us (2%)
  between operations  0.67 us (1%)
    pallas_call x1, Pallas kernels, finish(): pl.pallas_call(functools.partial(finish_kernel, PANEL, offsets, axes, sca...  23.2 us
    pallas_call x2, Pallas kernels, gram_sums(): pl.pallas_call(functools.partial(gram_kernel, groups, own, n // 2), in_sp...  12.4 us
    ppermute x1, waiting for transfers between devices, send_over(): lax.ppermute(x, 'tie', [(t, (t // 2 + hop) % pairs * 2 + t % 2) for t in...  6.05 us
    ppermute x1, starting transfers between devices, send_over(): lax.ppermute(x, 'tie', [(t, (t // 2 + hop) % pairs * 2 + t % 2) for t in...  2.87 us
    ppermute x2, starting transfers between devices, swap_cores(): return lax.ppermute(x, 'tie', [(t, t ^ 1) for t in range(n)])  1.76 us
    ppermute x2, waiting for transfers between devices, swap_cores(): return lax.ppermute(x, 'tie', [(t, t ^ 1) for t in range(n)])  1.56 us
  transfers between devices with their start and end apart: 3, of which 2 were waited for; matrix products, arithmetic and copies ran while one was open for 0% of the time, Pallas kernels for 13%

profile of v4, /device:TPU:0, one launch (start us, length us, event | category | flops | bytes accessed | tf_op | source)
XLA Modules:
  0.0 50.3 jit_solution(6535141765186321840)
XLA Ops:
  0.6 0.0 copy-start
  0.6 5.6 %shard_map.77 = (f32[4,264,128]{2,1,0:T(8,128)S(1)}, f32[4,264,128]{2,1,0:T(8,128)S(1)}) custom-call(s32[96]{0:T(128)} %counts.2, s32[16,96]{1,0:T(8,128)} %pattern.3, bf16[96,256,256]{2,1,0:T(8,128)(2,1)} %rows.3), custom_call_target="tpu_custom_call" | custom-call | tf_op jit(solution)/shard_map/pallas_call | solution.py:117
  6.3 1.6 %collective-permute-start = (f32[4,264,128]{2,1,0:T(8,128)S(1)}, f32[4,264,128]{2,1,0:T(8,128)S(1)}, u32[]{:S(2)}, u32[]{:S(2)}) collective-permute-start(f32[4,264,128]{2,1,0:T(8,128)S(1)} %get-tuple-element.11), channel_id=1, source_target_pairs={{0,1},{1,0},{2,3},{3,2},{4,5},{5,4},{6,7},{7,6},{8,9},{9,8},{10,11... | collective-permute-start | bytes 1622024 | tf_op jit(solution)/shard_map/ppermute | solution.py:133
  7.9 1.6 %collective-permute-done = f32[4,264,128]{2,1,0:T(8,128)S(1)} collective-permute-done((f32[4,264,128]{2,1,0:T(8,128)S(1)}, f32[4,264,128]{2,1,0:T(8,128)S(1)}, u32[]{:S(2)}, u32[]{:S(2)}) %collective-permute-start) | collective-permute-done | bytes 540704 | tf_op jit(solution)/shard_map/ppermute | solution.py:133
  9.4 0.9 %add.7 = f32[4,264,128]{2,1,0:T(8,128)} add(f32[4,264,128]{2,1,0:T(8,128)S(1)} %get-tuple-element.10, f32[4,264,128]{2,1,0:T(8,128)S(1)} %collective-permute-done) | non-fusion elementwise | flops 135168 | bytes 1622016 | tf_op jit(solution)/shard_map/add | solution.py:151
  10.3 0.0 copy-start.1
  10.3 0.0 copy-start.2
  10.3 2.9 %collective-permute-start.2 = (f32[4,264,128]{2,1,0:T(8,128)}, f32[4,264,128]{2,1,0:T(8,128)S(1)}, u32[]{:S(2)}, u32[]{:S(2)}) collective-permute-start(f32[4,264,128]{2,1,0:T(8,128)} %add.7), channel_id=1, source_target_pairs={{0,2},{1,3},{2,0},{3,1},{4,6},{5,7},{6,4},{7,5},{8,10},{9,11},{10,... | collective-permute-start | bytes 1622024 | tf_op jit(solution)/shard_map/ppermute | solution.py:138
  13.2 6.8 %shard_map.78 = (f32[4,264,128]{2,1,0:T(8,128)}, f32[4,264,128]{2,1,0:T(8,128)S(1)}) custom-call(s32[96]{0:T(128)} %counts.2, s32[16,96]{1,0:T(8,128)} %pattern.3, bf16[96,256,256]{2,1,0:T(8,128)(2,1)} %rows.3), custom_call_target="tpu_custom_call" | custom-call | tf_op jit(solution)/shard_map/pallas_call | solution.py:117
  19.9 0.1 collective-permute-start.1
  20.1 0.0 copy-done
  20.1 6.1 %collective-permute-done.2.rest_2_ = f32[4,264,128]{2,1,0:T(8,128)S(1)} collective-permute-done((f32[4,264,128]{2,1,0:T(8,128)}, f32[4,264,128]{2,1,0:T(8,128)S(1)}, u32[]{:S(2)}, u32[]{:S(2)}) %collective-permute-start.2) | collective-permute-done | bytes 540704 | tf_op jit(solution)/shard_map/ppermute | solution.py:138
  26.2 0.0 collective-permute-done.1.rest_1_
  26.2 0.0 copy-done.1
  26.2 0.0 copy-done.2
  26.2 23.2 %finish.1 = (f32[4,192,256]{2,1,0:T(8,128)S(1)}, f32[64,64]{1,0:T(8,128)S(1)}) custom-call(f32[4]{0:T(128)S(1)} %copy-done.1, bf16[4,192,192]{2,1,0:T(8,128)(2,1)S(1)} %constant_dynamic-slice_fusion.sens, f32[1,64]{1,0:T(1,128)S(1)} %bitcast.1, f32[4,264,128]{2,1,0:T(8,128)S(1)} %get-tuple-element.13.rest_0_, ...), custom_call_target="tpu_custom_call" | custom-call | tf_op jit(solution)/shard_map/finish/pallas_call | solution.py:354
  49.4 0.9 %emit.1 = (f32[4,192,256]{2,1,0:T(8,128)}, f32[64,64]{1,0:T(8,128)}) custom-call(f32[4,192,256]{2,1,0:T(8,128)S(1)} %get-tuple-element.16.rows, f32[64,64]{1,0:T(8,128)S(1)} %get-tuple-element.17.factor), custom_call_target="tpu_custom_call" | custom-call | tf_op jit(solution)/shard_map/emit/pallas_call | solution.py:398
  (1 shorter events, 0.0 us)
Async XLA Ops:
  0.6 19.5 %copy-start = (bf16[16,192,192]{2,1,0:T(8,128)(2,1)S(1)}, bf16[16,192,192]{2,1,0:T(8,128)(2,1)}, u32[]{:S(2)}) copy-start(bf16[16,192,192]{2,1,0:T(8,128)(2,1)} %param.9) | copy-start | bytes 3538948
  6.3 3.2 %collective-permute-start = (f32[4,264,128]{2,1,0:T(8,128)S(1)}, f32[4,264,128]{2,1,0:T(8,128)S(1)}, u32[]{:S(2)}, u32[]{:S(2)}) collective-permute-start(f32[4,264,128]{2,1,0:T(8,128)S(1)} %get-tuple-element.11), channel_id=1, source_target_pairs={{0,1},{1,0},{2,3},{3,2},{4,5},{5,4},{6,7},{7,6},{8,9},{9,8},{10,11... | collective-permute-start | bytes 1622024 | tf_op jit(solution)/shard_map/ppermute | solution.py:133
  10.3 15.9 %copy-start.1 = (f32[4]{0:T(128)S(1)}, f32[4]{0:T(128)}, u32[]{:S(2)}) copy-start(f32[4]{0:T(128)} %damping.1) | copy-start | bytes 52
  10.3 15.9 %copy-start.2 = (f32[64]{0:T(128)S(1)}, f32[64]{0:T(128)}, u32[]{:S(2)}) copy-start(f32[64]{0:T(128)} %param.11) | copy-start | bytes 772
  10.3 15.9 %collective-permute-start.2 = (f32[4,264,128]{2,1,0:T(8,128)}, f32[4,264,128]{2,1,0:T(8,128)S(1)}, u32[]{:S(2)}, u32[]{:S(2)}) collective-permute-start(f32[4,264,128]{2,1,0:T(8,128)} %add.7), channel_id=1, source_target_pairs={{0,2},{1,3},{2,0},{3,1},{4,6},{5,7},{6,4},{7,5},{8,10},{9,11},{10,... | collective-permute-start | bytes 1622024 | tf_op jit(solution)/shard_map/ppermute | solution.py:138
  19.9 6.2 %collective-permute-start.1 = (f32[4,264,128]{2,1,0:T(8,128)}, f32[4,264,128]{2,1,0:T(8,128)S(1)}, u32[]{:S(2)}, u32[]{:S(2)}) collective-permute-start(f32[4,264,128]{2,1,0:T(8,128)} %get-tuple-element.14), channel_id=1, source_target_pairs={{0,1},{1,0},{2,3},{3,2},{4,5},{5,4},{6,7},{7,6},{8,9},{9,8},{10,11... | collective-permute-start | bytes 1622024 | tf_op jit(solution)/shard_map/ppermute | solution.py:133
